TPU v7x, 768 devices: a whole 4x8x12 slice. The times are simulated.
768 devices in a mesh: grp: 8 (over y_lo, x), tile: 96 (over y_hi, z, core).
Axes of the slice: x: 4, y: 8 (y_hi: 4, y_lo: 2; y = y_hi * 2 + y_lo), z: 12, core: 2. Of those that a mesh axis runs over, the one named last changes fastest.
Arguments:
- ocean: float32 [4, 32, 32, 12288], P(None, None, 'grp', 'tile'), may hold values from -3 to 3
- tracers: bfloat16 [10, 32, 32, 12288], P(None, None, 'grp', 'tile'), may hold values from -6 to 6
- wet_blocks: int32 [8, 768], P('grp', 'tile'), may hold values 0 or 1
- surface_light: float32 [32, 12288], P('grp', 'tile'), may hold values from 0.5 to 1.5
- rates: float32 [10, 10], replicated, may hold values from -2 to 2
Outputs:
- ocean_out: float32 [4, 32, 32, 12288], P(None, None, 'grp', 'tile')
- tracer_out: bfloat16 [10, 32, 32, 12288], P(None, None, 'grp', 'tile')
- heating: float32 [32, 32, 12288], P(None, 'grp', 'tile')
All inputs are finite; a program needn't handle non-finite values. No bound on the sum of `wet_blocks` on one device may be relied on, other than what follows from the above.
Results may differ from a plain program's by a relative error of at most 0.0031.
Values may be sent and summed in bfloat16 or wider, within the bound.
No kernel may reach another device: no remote copies, remote signals or barrier semaphores. Data moves between devices by JAX's collectives and lax.ppermute only.
A program may use at most 32 MiB of HBM per device.

v0:
```python
import jax
import jax.numpy as jnp
from jax import lax
from jax.sharding import PartitionSpec as P

WBY = 4
WBX = 16


time_step = 0.3
coriolis = 0.2
viscosity = 0.1
diffusion = 0.05
thermal = 0.2
haline = 0.15
gravity_red = 0.05
react_step = 0.5
water_atten = 0.3
chloro_atten = 0.2


def extended(array, sides, width):
    for axis, dim in sides:
        devices, length = (lax.axis_size(axis), array.shape[dim])
        up = [(i, (i + 1) % devices) for i in range(devices - 1)]
        down = [(j, i) for i, j in up]
        last = lax.slice_in_dim(array, length - width, length, axis=dim)
        first = lax.slice_in_dim(array, 0, width, axis=dim)
        before = lax.ppermute(last, axis, up)
        after = lax.ppermute(first, axis, down)
        array = jnp.concatenate([before, array, after], axis=dim)
    return array


def minmod(first, second):
    return 0.5 * (jnp.sign(first) + jnp.sign(second)) * jnp.minimum(jnp.abs(first), jnp.abs(second))


def ocean_tendency(padded):
    center = padded[:, :, 2:-2, 2:-2]
    east_side = padded[:, :, 2:-2, 3:-1]
    west_side = padded[:, :, 2:-2, 1:-3]
    north_side = padded[:, :, 3:-1, 2:-2]
    south_side = padded[:, :, 1:-3, 2:-2]
    grad_x = 0.5 * (east_side - west_side)
    grad_y = 0.5 * (north_side - south_side)
    laplace = east_side + west_side + north_side + south_side - 4.0 * center
    zonal_vel = center[0]
    merid_vel = center[1]
    advect = -(zonal_vel[None] * grad_x + merid_vel[None] * grad_y)
    press_x = gravity_red * jnp.cumsum(thermal * grad_x[2] - haline * grad_x[3], axis=0)
    press_y = gravity_red * jnp.cumsum(thermal * grad_y[2] - haline * grad_y[3], axis=0)
    zonal_rate = advect[0] + coriolis * merid_vel - press_x + viscosity * laplace[0]
    merid_rate = advect[1] - coriolis * zonal_vel - press_y + viscosity * laplace[1]
    heat_rate = advect[2] + diffusion * laplace[2]
    salt_rate = advect[3] + diffusion * laplace[3]
    return jnp.stack([zonal_rate, merid_rate, heat_rate, salt_rate], 0)


def limited_divergence(cells, speeds, axis):
    count = cells.shape[axis] - 4

    def part(source, start, length):
        return lax.slice_in_dim(source, start, start + length, axis=axis)

    face_speed = 0.5 * (part(speeds, 1, count + 1) + part(speeds, 2, count + 1))
    behind = part(cells, 0, count + 1)
    inside = part(cells, 1, count + 1)
    ahead = part(cells, 2, count + 1)
    beyond = part(cells, 3, count + 1)
    left_value = inside + 0.5 * minmod(inside - behind, ahead - inside)
    right_value = ahead - 0.5 * minmod(ahead - inside, beyond - ahead)
    flux = jnp.maximum(face_speed, 0.0) * left_value + jnp.minimum(face_speed, 0.0) * right_value
    return part(flux, 1, count) - part(flux, 0, count)


def tracer_tendency(cells, padded_ocean):
    zonal_row = padded_ocean[0:1, :, 2:-2, :]
    merid_col = padded_ocean[1:2, :, :, 2:-2]
    along_x = limited_divergence(cells[:, :, 2:-2, :], zonal_row, 3)
    along_y = limited_divergence(cells[:, :, :, 2:-2], merid_col, 2)
    return -(along_x + along_y)


def expand_mask(wet_blocks):
    blocks = wet_blocks.astype(jnp.float32)
    rows, cols = blocks.shape
    wide = jnp.broadcast_to(blocks[:, None, :, None], (rows, WBY, cols, WBX))
    return wide.reshape(rows * WBY, cols * WBX)


def section_rims(ocean_state, tracer_state):
    padded_ocean = extended(ocean_state, (("grp", 2), ("tile", 3)), 2)
    padded_tracer = extended(tracer_state, (("grp", 2), ("tile", 3)), 2).astype(jnp.float32)
    return (ocean_tendency(padded_ocean), tracer_tendency(padded_tracer, padded_ocean))


def shards(ocean, tracers, wet_blocks, surface_light, rates):
    start = tracers.astype(jnp.float32)
    ocean_rate, tracer_rate = section_rims(ocean, tracers)
    ocean_one = ocean + time_step * ocean_rate
    tracer_one = lax.optimization_barrier((start + time_step * tracer_rate).astype(jnp.bfloat16))
    ocean_rate, tracer_rate = section_rims(ocean_one, tracer_one)
    tracer_mid = tracer_one.astype(jnp.float32)
    ocean_two = 0.5 * (ocean + ocean_one + time_step * ocean_rate)
    tracer_two = 0.5 * (start + tracer_mid + time_step * tracer_rate)
    wet_cells = expand_mask(wet_blocks)
    reaction = jnp.einsum("ab,bzyx->azyx", rates, tracer_two, precision=lax.Precision.HIGHEST)
    reacted = tracer_two + react_step * wet_cells * reaction
    attenuation = water_atten + chloro_atten * reacted[0] * reacted[0]
    depth_sum = jnp.cumsum(attenuation, axis=0)
    heating = wet_cells * surface_light * (jnp.exp(attenuation - depth_sum) - jnp.exp(-depth_sum))
    ocean_out = jnp.concatenate(
        [ocean_two[:2], ocean_two[2:3] + time_step * heating[None], ocean_two[3:]], 0
    )
    return (ocean_out, reacted.astype(jnp.bfloat16), heating)


def solution(mesh):
    return jax.shard_map(
        shards,
        mesh=mesh,
        in_specs=(
            P(None, None, "grp", "tile"),
            P(None, None, "grp", "tile"),
            P("grp", "tile"),
            P("grp", "tile"),
            P(),
        ),
        out_specs=(
            P(None, None, "grp", "tile"),
            P(None, None, "grp", "tile"),
            P(None, "grp", "tile"),
        ),
        check_vma=False,
    )
```

profile of v0, /device:TPU:40, one launch (start us, length us, event | category | flops | bytes accessed | tf_op | source)
XLA Modules:
  0.0 127.6 jit_solution(11563624902672596675)
XLA Ops:
  1.7 5.6 %collective-permute-start.1 = (f32[4,32,2,128]{3,1,2,0:T(8,128)S(1)}, f32[4,32,2,128]{3,1,2,0:T(8,128)S(1)}, u32[]{:S(2)}, u32[]{:S(2)}) collective-permute-start(f32[4,32,2,128]{3,1,2,0:T(8,128)S(1)} %get-tuple-element.68), channel_id=1, source_target_pairs={{96,0},{192,96},{288,192},{384,288},{480,384},{576,480},{672,576},... | collective-permute-start | bytes 393224 | tf_op jit(solution)/shard_map/ppermute | solution.py:30
  7.3 1.9 %collective-permute-start = (f32[4,32,2,128]{3,1,2,0:T(8,128)S(1)}, f32[4,32,2,128]{3,1,2,0:T(8,128)S(1)}, u32[]{:S(2)}, u32[]{:S(2)}) collective-permute-start(f32[4,32,2,128]{3,1,2,0:T(8,128)S(1)} %get-tuple-element.69), channel_id=1, source_target_pairs={{0,96},{96,192},{192,288},{288,384},{384,480},{480,576},{576,672},... | collective-permute-start | bytes 393224 | tf_op jit(solution)/shard_map/ppermute | solution.py:29
  10.7 1.9 %collective-permute-start.8 = (bf16[10,32,2,128]{3,1,2,0:T(8,128)(2,1)S(1)}, bf16[10,32,2,128]{3,1,2,0:T(8,128)(2,1)S(1)}, u32[]{:S(2)}, u32[]{:S(2)}) collective-permute-start(bf16[10,32,2,128]{3,1,2,0:T(8,128)(2,1)S(1)} %copy.184), channel_id=1, source_target_pairs={{0,96},{96,192},{192,288},{288,384},{384,480},{480,576},{576,672},... | collective-permute-start | bytes 491528 | tf_op jit(solution)/shard_map/ppermute | solution.py:29
  12.6 6.0 %collective-permute-start.9 = (bf16[10,32,2,128]{3,1,2,0:T(8,128)(2,1)S(1)}, bf16[10,32,2,128]{3,1,2,0:T(8,128)(2,1)S(1)}, u32[]{:S(2)}, u32[]{:S(2)}) collective-permute-start(bf16[10,32,2,128]{3,1,2,0:T(8,128)(2,1)S(1)} %copy.185), channel_id=1, source_target_pairs={{96,0},{192,96},{288,192},{384,288},{480,384},{576,480},{672,576},... | collective-permute-start | bytes 491528 | tf_op jit(solution)/shard_map/ppermute | solution.py:30
  19.3 13.0 %collective-permute-start.2 = (f32[4,32,8,2]{3,1,2,0:T(8,128)S(1)}, f32[4,32,8,2]{3,1,2,0:T(8,128)S(1)}, u32[]{:S(2)}, u32[]{:S(2)}) collective-permute-start(f32[4,32,8,2]{3,1,2,0:T(8,128)S(1)} %get-tuple-element.51), channel_id=1, source_target_pairs={{1,0},{2,1},{3,2},{4,3},{5,4},{6,5},{7,6},{8,7},{9,8},{10,9},{11,1... | collective-permute-start | bytes 24584 | tf_op jit(solution)/shard_map/ppermute | solution.py:30
  32.2 1.9 %collective-permute-start.3 = (f32[4,32,8,2]{3,1,2,0:T(8,128)S(1)}, f32[4,32,8,2]{3,1,2,0:T(8,128)S(1)}, u32[]{:S(2)}, u32[]{:S(2)}) collective-permute-start(f32[4,32,8,2]{3,1,2,0:T(8,128)S(1)} %get-tuple-element.52), channel_id=1, source_target_pairs={{0,1},{1,2},{2,3},{3,4},{4,5},{5,6},{6,7},{7,8},{8,9},{9,10},{10,1... | collective-permute-start | bytes 24584 | tf_op jit(solution)/shard_map/ppermute | solution.py:29
  34.9 6.8 %collective-permute-done.2 = f32[4,32,8,2]{3,1,2,0:T(8,128)S(1)} collective-permute-done((f32[4,32,8,2]{3,1,2,0:T(8,128)S(1)}, f32[4,32,8,2]{3,1,2,0:T(8,128)S(1)}, u32[]{:S(2)}, u32[]{:S(2)}) %collective-permute-start.2) | collective-permute-done | bytes 8224 | tf_op jit(solution)/shard_map/ppermute | solution.py:30
  41.7 7.4 %collective-permute-done.3 = f32[4,32,8,2]{3,1,2,0:T(8,128)S(1)} collective-permute-done((f32[4,32,8,2]{3,1,2,0:T(8,128)S(1)}, f32[4,32,8,2]{3,1,2,0:T(8,128)S(1)}, u32[]{:S(2)}, u32[]{:S(2)}) %collective-permute-start.3) | collective-permute-done | bytes 8224 | tf_op jit(solution)/shard_map/ppermute | solution.py:29
  53.2 1.9 %collective-permute-start.11 = (bf16[10,32,8,2]{1,2,3,0:T(8,128)(2,1)S(1)}, bf16[10,32,8,2]{1,2,3,0:T(8,128)(2,1)S(1)}, u32[]{:S(2)}, u32[]{:S(2)}) collective-permute-start(bf16[10,32,8,2]{1,2,3,0:T(8,128)(2,1)S(1)} %copy.127), channel_id=1, source_target_pairs={{1,0},{2,1},{3,2},{4,3},{5,4},{6,5},{7,6},{8,7},{9,8},{10,9},{11,1... | collective-permute-start | bytes 30728 | tf_op jit(solution)/shard_map/ppermute | solution.py:30
  55.1 2.4 %collective-permute-start.10 = (bf16[10,32,8,2]{1,2,3,0:T(8,128)(2,1)S(1)}, bf16[10,32,8,2]{1,2,3,0:T(8,128)(2,1)S(1)}, u32[]{:S(2)}, u32[]{:S(2)}) collective-permute-start(bf16[10,32,8,2]{1,2,3,0:T(8,128)(2,1)S(1)} %copy.126), channel_id=1, source_target_pairs={{0,1},{1,2},{2,3},{3,4},{4,5},{5,6},{6,7},{7,8},{8,9},{9,10},{10,1... | collective-permute-start | bytes 30728 | tf_op jit(solution)/shard_map/ppermute | solution.py:29
  58.2 3.1 %collective-permute-start.4 = (f32[4,32,2,128]{3,1,2,0:T(8,128)}, f32[4,32,2,128]{3,1,2,0:T(8,128)S(1)}, u32[]{:S(2)}, u32[]{:S(2)}) collective-permute-start(f32[4,32,2,128]{3,1,2,0:T(8,128)} %get-tuple-element.61), channel_id=1, source_target_pairs={{0,96},{96,192},{192,288},{288,384},{384,480},{480,576},{576,672},... | collective-permute-start | bytes 393224 | tf_op jit(solution)/shard_map/ppermute | solution.py:29
  61.3 4.9 %collective-permute-start.5 = (f32[4,32,2,128]{3,1,2,0:T(8,128)}, f32[4,32,2,128]{3,1,2,0:T(8,128)S(1)}, u32[]{:S(2)}, u32[]{:S(2)}) collective-permute-start(f32[4,32,2,128]{3,1,2,0:T(8,128)} %get-tuple-element.62), channel_id=1, source_target_pairs={{96,0},{192,96},{288,192},{384,288},{480,384},{576,480},{672,576},... | collective-permute-start | bytes 393224 | tf_op jit(solution)/shard_map/ppermute | solution.py:30
  69.6 2.0 %multiply_add_fusion.1 = f32[10,32,4,129]{3,1,2,0:T(8,128)S(1)} fusion(f32[10,32,8,132]{3,1,2,0:T(8,128)S(1)} %maximum_convert_fusion, f32[32,4,129]{2,0,1:T(8,128)S(1)} %copy-done.3, f32[32,4,129]{2,0,1:T(8,128)S(1)} %get-tuple-element.21), kind=kLoop, calls=%fused_computation.7 | loop fusion | flops 3962880 | bytes 3434496 | tf_op jit(solution)/shard_map/add | solution.py:73
  71.8 1.9 %collective-permute-start.12 = (bf16[10,32,2,128]{3,1,2,0:T(8,128)(2,1)S(1)}, bf16[10,32,2,128]{3,1,2,0:T(8,128)(2,1)S(1)}, u32[]{:S(2)}, u32[]{:S(2)}) collective-permute-start(bf16[10,32,2,128]{3,1,2,0:T(8,128)(2,1)S(1)} %get-tuple-element.53), channel_id=1, source_target_pairs={{0,96},{96,192},{192,288},{288,384},{384,480},{480,576},{576,672},... | collective-permute-start | bytes 491528 | tf_op jit(solution)/shard_map/ppermute | solution.py:29
  73.8 6.0 %collective-permute-start.13 = (bf16[10,32,2,128]{3,1,2,0:T(8,128)(2,1)S(1)}, bf16[10,32,2,128]{3,1,2,0:T(8,128)(2,1)S(1)}, u32[]{:S(2)}, u32[]{:S(2)}) collective-permute-start(bf16[10,32,2,128]{3,1,2,0:T(8,128)(2,1)S(1)} %get-tuple-element.54), channel_id=1, source_target_pairs={{96,0},{192,96},{288,192},{384,288},{480,384},{576,480},{672,576},... | collective-permute-start | bytes 491528 | tf_op jit(solution)/shard_map/ppermute | solution.py:30
  80.1 6.3 %collective-permute-start.6 = (f32[4,32,8,2]{3,1,2,0:T(8,128)S(1)}, f32[4,32,8,2]{3,1,2,0:T(8,128)S(1)}, u32[]{:S(2)}, u32[]{:S(2)}) collective-permute-start(f32[4,32,8,2]{3,1,2,0:T(8,128)S(1)} %get-tuple-element.47), channel_id=1, source_target_pairs={{1,0},{2,1},{3,2},{4,3},{5,4},{6,5},{7,6},{8,7},{9,8},{10,9},{11,1... | collective-permute-start | bytes 24584 | tf_op jit(solution)/shard_map/ppermute | solution.py:30
  86.3 1.9 %collective-permute-start.7 = (f32[4,32,8,2]{3,1,2,0:T(8,128)S(1)}, f32[4,32,8,2]{3,1,2,0:T(8,128)S(1)}, u32[]{:S(2)}, u32[]{:S(2)}) collective-permute-start(f32[4,32,8,2]{3,1,2,0:T(8,128)S(1)} %get-tuple-element.48), channel_id=1, source_target_pairs={{0,1},{1,2},{2,3},{3,4},{4,5},{5,6},{6,7},{7,8},{8,9},{9,10},{10,1... | collective-permute-start | bytes 24584 | tf_op jit(solution)/shard_map/ppermute | solution.py:29
  89.0 5.2 %collective-permute-done.6 = f32[4,32,8,2]{3,1,2,0:T(8,128)S(1)} collective-permute-done((f32[4,32,8,2]{3,1,2,0:T(8,128)S(1)}, f32[4,32,8,2]{3,1,2,0:T(8,128)S(1)}, u32[]{:S(2)}, u32[]{:S(2)}) %collective-permute-start.6) | collective-permute-done | bytes 8224 | tf_op jit(solution)/shard_map/ppermute | solution.py:30
  94.2 9.2 %collective-permute-done.7 = f32[4,32,8,2]{3,1,2,0:T(8,128)S(1)} collective-permute-done((f32[4,32,8,2]{3,1,2,0:T(8,128)S(1)}, f32[4,32,8,2]{3,1,2,0:T(8,128)S(1)}, u32[]{:S(2)}, u32[]{:S(2)}) %collective-permute-start.7) | collective-permute-done | bytes 8224 | tf_op jit(solution)/shard_map/ppermute | solution.py:29
  105.8 1.9 %collective-permute-start.15 = (bf16[10,32,8,2]{1,2,3,0:T(8,128)(2,1)S(1)}, bf16[10,32,8,2]{1,2,3,0:T(8,128)(2,1)S(1)}, u32[]{:S(2)}, u32[]{:S(2)}) collective-permute-start(bf16[10,32,8,2]{1,2,3,0:T(8,128)(2,1)S(1)} %copy.131), channel_id=1, source_target_pairs={{1,0},{2,1},{3,2},{4,3},{5,4},{6,5},{7,6},{8,7},{9,8},{10,9},{11,1... | collective-permute-start | bytes 30728 | tf_op jit(solution)/shard_map/ppermute | solution.py:30
  107.7 2.6 %collective-permute-start.14 = (bf16[10,32,8,2]{1,2,3,0:T(8,128)(2,1)S(1)}, bf16[10,32,8,2]{1,2,3,0:T(8,128)(2,1)S(1)}, u32[]{:S(2)}, u32[]{:S(2)}) collective-permute-start(bf16[10,32,8,2]{1,2,3,0:T(8,128)(2,1)S(1)} %copy.130), channel_id=1, source_target_pairs={{0,1},{1,2},{2,3},{3,4},{4,5},{5,6},{6,7},{7,8},{8,9},{9,10},{10,1... | collective-permute-start | bytes 30728 | tf_op jit(solution)/shard_map/ppermute | solution.py:29
  110.3 6.9 %collective-permute-done.14 = bf16[10,32,8,2]{1,2,3,0:T(8,128)(2,1)S(1)} collective-permute-done((bf16[10,32,8,2]{1,2,3,0:T(8,128)(2,1)S(1)}, bf16[10,32,8,2]{1,2,3,0:T(8,128)(2,1)S(1)}, u32[]{:S(2)}, u32[]{:S(2)}) %collective-permute-start.14) | collective-permute-done | bytes 10272 | tf_op jit(solution)/shard_map/ppermute | solution.py:29
  120.6 2.0 %multiply_add_fusion = f32[10,32,4,129]{3,1,2,0:T(8,128)S(1)} fusion(f32[10,32,8,132]{3,1,2,0:T(8,128)S(1)} %maximum_convert_fusion.1, f32[32,4,129]{2,0,1:T(8,128)S(1)} %minimum_bitcast_fusion, f32[32,4,129]{2,0,1:T(8,128)S(1)} %get-tuple-element.17), kind=kLoop, calls=%fused_computation.6 | loop fusion | flops 3962880 | bytes 3434496 | tf_op jit(solution)/shard_map/add | solution.py:73
  123.0 1.5 %fusion = f32[32,4,128,10]{2,3,1,0:T(8,128)S(1)} fusion(f32[10,32,4,128]{3,1,2,0:T(8,128)S(1)} %fusion.4, f32[10,10]{1,0:T(8,128)S(1)} %copy-done), kind=kOutput, calls=%fused_computation.8 | convolution fusion | flops 19660800 | bytes 1311120 | tf_op jit(solution)/shard_map/ab,bzyx->azyx/dot_general | solution.py:108
  (105 shorter events, 22.0 us)
Async XLA Ops:
  0.6 122.3 %copy-start = (f32[10,10]{1,0:T(8,128)S(1)}, f32[10,10]{1,0:T(8,128)}, u32[]{:S(2)}) copy-start(f32[10,10]{1,0:T(8,128)} %param.9) | copy-start | bytes 1204
  0.6 18.1 %copy-start.10 = (s32[1,8]{1,0:T(1,128)S(1)}, s32[1,8]{1,0:T(1,128)}, u32[]{:S(2)}) copy-start(s32[1,8]{1,0:T(1,128)} %param.7) | copy-start | bytes 100
  0.7 18.2 %copy-start.9 = (f32[4,128]{1,0:T(4,128)S(1)}, f32[4,128]{1,0:T(4,128)}, u32[]{:S(2)}) copy-start(f32[4,128]{1,0:T(4,128)} %param.8) | copy-start | bytes 6148
  1.7 17.3 %copy-start.1 = (f32[4,32,4,128]{3,2,1,0:T(4,128)S(1)}, f32[4,32,4,128]{3,2,1,0:T(4,128)}, u32[]{:S(2)}) copy-start(f32[4,32,4,128]{3,2,1,0:T(4,128)} %param.5) | copy-start | bytes 786436
  1.7 17.3 %collective-permute-start.1 = (f32[4,32,2,128]{3,1,2,0:T(8,128)S(1)}, f32[4,32,2,128]{3,1,2,0:T(8,128)S(1)}, u32[]{:S(2)}, u32[]{:S(2)}) collective-permute-start(f32[4,32,2,128]{3,1,2,0:T(8,128)S(1)} %get-tuple-element.68), channel_id=1, source_target_pairs={{96,0},{192,96},{288,192},{384,288},{480,384},{576,480},{672,576},... | collective-permute-start | bytes 393224 | tf_op jit(solution)/shard_map/ppermute | solution.py:30
  7.3 11.6 %collective-permute-start = (f32[4,32,2,128]{3,1,2,0:T(8,128)S(1)}, f32[4,32,2,128]{3,1,2,0:T(8,128)S(1)}, u32[]{:S(2)}, u32[]{:S(2)}) collective-permute-start(f32[4,32,2,128]{3,1,2,0:T(8,128)S(1)} %get-tuple-element.69), channel_id=1, source_target_pairs={{0,96},{96,192},{192,288},{288,384},{384,480},{480,576},{576,672},... | collective-permute-start | bytes 393224 | tf_op jit(solution)/shard_map/ppermute | solution.py:29
  10.7 40.8 %collective-permute-start.8 = (bf16[10,32,2,128]{3,1,2,0:T(8,128)(2,1)S(1)}, bf16[10,32,2,128]{3,1,2,0:T(8,128)(2,1)S(1)}, u32[]{:S(2)}, u32[]{:S(2)}) collective-permute-start(bf16[10,32,2,128]{3,1,2,0:T(8,128)(2,1)S(1)} %copy.184), channel_id=1, source_target_pairs={{0,96},{96,192},{192,288},{288,384},{384,480},{480,576},{576,672},... | collective-permute-start | bytes 491528 | tf_op jit(solution)/shard_map/ppermute | solution.py:29
  12.6 39.1 %collective-permute-start.9 = (bf16[10,32,2,128]{3,1,2,0:T(8,128)(2,1)S(1)}, bf16[10,32,2,128]{3,1,2,0:T(8,128)(2,1)S(1)}, u32[]{:S(2)}, u32[]{:S(2)}) collective-permute-start(bf16[10,32,2,128]{3,1,2,0:T(8,128)(2,1)S(1)} %copy.185), channel_id=1, source_target_pairs={{96,0},{192,96},{288,192},{384,288},{480,384},{576,480},{672,576},... | collective-permute-start | bytes 491528 | tf_op jit(solution)/shard_map/ppermute | solution.py:30
  19.3 22.4 %collective-permute-start.2 = (f32[4,32,8,2]{3,1,2,0:T(8,128)S(1)}, f32[4,32,8,2]{3,1,2,0:T(8,128)S(1)}, u32[]{:S(2)}, u32[]{:S(2)}) collective-permute-start(f32[4,32,8,2]{3,1,2,0:T(8,128)S(1)} %get-tuple-element.51), channel_id=1, source_target_pairs={{1,0},{2,1},{3,2},{4,3},{5,4},{6,5},{7,6},{8,7},{9,8},{10,9},{11,1... | collective-permute-start | bytes 24584 | tf_op jit(solution)/shard_map/ppermute | solution.py:30
  32.2 16.9 %collective-permute-start.3 = (f32[4,32,8,2]{3,1,2,0:T(8,128)S(1)}, f32[4,32,8,2]{3,1,2,0:T(8,128)S(1)}, u32[]{:S(2)}, u32[]{:S(2)}) collective-permute-start(f32[4,32,8,2]{3,1,2,0:T(8,128)S(1)} %get-tuple-element.52), channel_id=1, source_target_pairs={{0,1},{1,2},{2,3},{3,4},{4,5},{5,6},{6,7},{7,8},{8,9},{9,10},{10,1... | collective-permute-start | bytes 24584 | tf_op jit(solution)/shard_map/ppermute | solution.py:29
  50.7 1.0 copy-start.2
  53.2 13.6 %collective-permute-start.11 = (bf16[10,32,8,2]{1,2,3,0:T(8,128)(2,1)S(1)}, bf16[10,32,8,2]{1,2,3,0:T(8,128)(2,1)S(1)}, u32[]{:S(2)}, u32[]{:S(2)}) collective-permute-start(bf16[10,32,8,2]{1,2,3,0:T(8,128)(2,1)S(1)} %copy.127), channel_id=1, source_target_pairs={{1,0},{2,1},{3,2},{4,3},{5,4},{6,5},{7,6},{8,7},{9,8},{10,9},{11,1... | collective-permute-start | bytes 30728 | tf_op jit(solution)/shard_map/ppermute | solution.py:30
  55.1 11.0 %collective-permute-start.10 = (bf16[10,32,8,2]{1,2,3,0:T(8,128)(2,1)S(1)}, bf16[10,32,8,2]{1,2,3,0:T(8,128)(2,1)S(1)}, u32[]{:S(2)}, u32[]{:S(2)}) collective-permute-start(bf16[10,32,8,2]{1,2,3,0:T(8,128)(2,1)S(1)} %copy.126), channel_id=1, source_target_pairs={{0,1},{1,2},{2,3},{3,4},{4,5},{5,6},{6,7},{7,8},{8,9},{9,10},{10,1... | collective-permute-start | bytes 30728 | tf_op jit(solution)/shard_map/ppermute | solution.py:29
  58.2 21.6 %collective-permute-start.4 = (f32[4,32,2,128]{3,1,2,0:T(8,128)}, f32[4,32,2,128]{3,1,2,0:T(8,128)S(1)}, u32[]{:S(2)}, u32[]{:S(2)}) collective-permute-start(f32[4,32,2,128]{3,1,2,0:T(8,128)} %get-tuple-element.61), channel_id=1, source_target_pairs={{0,96},{96,192},{192,288},{288,384},{384,480},{480,576},{576,672},... | collective-permute-start | bytes 393224 | tf_op jit(solution)/shard_map/ppermute | solution.py:29
  61.3 18.6 %collective-permute-start.5 = (f32[4,32,2,128]{3,1,2,0:T(8,128)}, f32[4,32,2,128]{3,1,2,0:T(8,128)S(1)}, u32[]{:S(2)}, u32[]{:S(2)}) collective-permute-start(f32[4,32,2,128]{3,1,2,0:T(8,128)} %get-tuple-element.62), channel_id=1, source_target_pairs={{96,0},{192,96},{288,192},{384,288},{480,384},{576,480},{672,576},... | collective-permute-start | bytes 393224 | tf_op jit(solution)/shard_map/ppermute | solution.py:30
  68.3 1.3 %copy-start.3 = (f32[32,4,129]{2,0,1:T(8,128)S(1)}, f32[32,4,129]{2,0,1:T(8,128)}, u32[]{:S(2)}) copy-start(f32[32,4,129]{2,0,1:T(8,128)} %minimum_bitcast_fusion.1) | copy-start | bytes 198148
  71.8 32.4 %collective-permute-start.12 = (bf16[10,32,2,128]{3,1,2,0:T(8,128)(2,1)S(1)}, bf16[10,32,2,128]{3,1,2,0:T(8,128)(2,1)S(1)}, u32[]{:S(2)}, u32[]{:S(2)}) collective-permute-start(bf16[10,32,2,128]{3,1,2,0:T(8,128)(2,1)S(1)} %get-tuple-element.53), channel_id=1, source_target_pairs={{0,96},{96,192},{192,288},{288,384},{384,480},{480,576},{576,672},... | collective-permute-start | bytes 491528 | tf_op jit(solution)/shard_map/ppermute | solution.py:29
  73.8 30.5 %collective-permute-start.13 = (bf16[10,32,2,128]{3,1,2,0:T(8,128)(2,1)S(1)}, bf16[10,32,2,128]{3,1,2,0:T(8,128)(2,1)S(1)}, u32[]{:S(2)}, u32[]{:S(2)}) collective-permute-start(bf16[10,32,2,128]{3,1,2,0:T(8,128)(2,1)S(1)} %get-tuple-element.54), channel_id=1, source_target_pairs={{96,0},{192,96},{288,192},{384,288},{480,384},{576,480},{672,576},... | collective-permute-start | bytes 491528 | tf_op jit(solution)/shard_map/ppermute | solution.py:30
  80.1 14.1 %collective-permute-start.6 = (f32[4,32,8,2]{3,1,2,0:T(8,128)S(1)}, f32[4,32,8,2]{3,1,2,0:T(8,128)S(1)}, u32[]{:S(2)}, u32[]{:S(2)}) collective-permute-start(f32[4,32,8,2]{3,1,2,0:T(8,128)S(1)} %get-tuple-element.47), channel_id=1, source_target_pairs={{1,0},{2,1},{3,2},{4,3},{5,4},{6,5},{7,6},{8,7},{9,8},{10,9},{11,1... | collective-permute-start | bytes 24584 | tf_op jit(solution)/shard_map/ppermute | solution.py:30
  86.3 17.0 %collective-permute-start.7 = (f32[4,32,8,2]{3,1,2,0:T(8,128)S(1)}, f32[4,32,8,2]{3,1,2,0:T(8,128)S(1)}, u32[]{:S(2)}, u32[]{:S(2)}) collective-permute-start(f32[4,32,8,2]{3,1,2,0:T(8,128)S(1)} %get-tuple-element.48), channel_id=1, source_target_pairs={{0,1},{1,2},{2,3},{3,4},{4,5},{5,6},{6,7},{7,8},{8,9},{9,10},{10,1... | collective-permute-start | bytes 24584 | tf_op jit(solution)/shard_map/ppermute | solution.py:29
  88.9 14.9 %copy-start.7 = (f32[32,4,128]{2,0,1:T(8,128)S(1)}, f32[32,4,128]{2,0,1:T(8,128)}, u32[]{:S(2)}) copy-start(f32[32,4,128]{2,0,1:T(8,128)} %get-tuple-element.59) | copy-start | bytes 196612
  88.9 14.9 %copy-start.8 = (f32[32,4,128]{2,0,1:T(8,128)S(1)}, f32[32,4,128]{2,0,1:T(8,128)}, u32[]{:S(2)}) copy-start(f32[32,4,128]{2,0,1:T(8,128)} %get-tuple-element.60) | copy-start | bytes 196612
  105.8 12.1 %collective-permute-start.15 = (bf16[10,32,8,2]{1,2,3,0:T(8,128)(2,1)S(1)}, bf16[10,32,8,2]{1,2,3,0:T(8,128)(2,1)S(1)}, u32[]{:S(2)}, u32[]{:S(2)}) collective-permute-start(bf16[10,32,8,2]{1,2,3,0:T(8,128)(2,1)S(1)} %copy.131), channel_id=1, source_target_pairs={{1,0},{2,1},{3,2},{4,3},{5,4},{6,5},{7,6},{8,7},{9,8},{10,9},{11,1... | collective-permute-start | bytes 30728 | tf_op jit(solution)/shard_map/ppermute | solution.py:30
  107.7 9.5 %collective-permute-start.14 = (bf16[10,32,8,2]{1,2,3,0:T(8,128)(2,1)S(1)}, bf16[10,32,8,2]{1,2,3,0:T(8,128)(2,1)S(1)}, u32[]{:S(2)}, u32[]{:S(2)}) collective-permute-start(bf16[10,32,8,2]{1,2,3,0:T(8,128)(2,1)S(1)} %copy.130), channel_id=1, source_target_pairs={{0,1},{1,2},{2,3},{3,4},{4,5},{5,6},{6,7},{7,8},{8,9},{9,10},{10,1... | collective-permute-start | bytes 30728 | tf_op jit(solution)/shard_map/ppermute | solution.py:29
  (3 other events, 2.7 us)
where the time goes:
time: 128 us
  starting transfers between devices  63.2 us (49%)
  waiting for transfers between devices  35.6 us (28%)
  other arithmetic  13.7 us (11%)
  local copies, waits for them, and re-layouts  12.2 us (10%)
  matrix products  1.54 us (1%)
  between operations  1.32 us (1%)
    ppermute x8, starting transfers between devices, extended(): after = lax.ppermute(first, axis, down)  45.6 us
    ppermute x8, waiting for transfers between devices, extended(): before = lax.ppermute(last, axis, up)  23.5 us
    ppermute x8, starting transfers between devices, extended(): before = lax.ppermute(last, axis, up)  17.7 us
    ppermute x8, waiting for transfers between devices, extended(): after = lax.ppermute(first, axis, down)  12.1 us
    add x4, other arithmetic, limited_divergence(): jnp.maximum(face_speed, 0.0) * left_value  6.47 us
    unnamed x32, local copies, waits for them, and re-layouts  4.23 us
    slice x6, local copies, waits for them, and re-layouts, extended(): first = lax.slice_in_dim(array, 0, width, axis=dim)  2.99 us
  transfers between devices with their start and end apart: 16, of which 5 were waited for; matrix products, arithmetic and copies ran while one was open for 11% of the time, Pallas kernels for 0%

commit v1 on v0

v1 whole, which is shorter than its diff:
```python
import functools

import jax
import jax.numpy as jnp
from jax import lax
from jax.experimental import pallas as pl
from jax.experimental.pallas import tpu as pltpu
from jax.sharding import PartitionSpec as P

LEVELS = 32
ROWS = 4
LANES = 128
BLOCKS = LEVELS // 8
GROUP = 24
COPIES = 5
TRACERS = 10

time_step = 0.3
coriolis = 0.2
viscosity = 0.1
diffusion = 0.05
thermal = 0.2
haline = 0.15
gravity_red = 0.05
react_step = 0.5
water_atten = 0.3
chloro_atten = 0.2

U, V, T, S = range(4)
FACES = {}
_count = 0
for _name, _first, _number in (
    ("up1", -2, 8),
    ("um1", -2, 8),
    ("vp1", -3, 9),
    ("vm1", -3, 9),
    ("up2", 0, 4),
    ("um2", 0, 4),
    ("vp2", -1, 5),
    ("vm2", -1, 5),
):
    FACES[_name] = (_count, _first)
    _count += _number
FACE_SLOTS = _count


def roll(x, shift, axis=1):
    return pltpu.roll(x, shift % x.shape[axis], axis)


def east(x):
    return roll(x, -1)


def west(x):
    return roll(x, 1)


def half_minmod(a, b):
    return 0.5 * jnp.maximum(jnp.minimum(a, b), jnp.minimum(jnp.maximum(a, b), 0.0))


def rows_of(block, y):
    return pl.ds(block * 8 * ROWS + y, 8, stride=ROWS)


def running_sum(x, sub):
    for step in (1, 2, 4):
        x = x + jnp.where(sub >= step, roll(x, step, 0), 0.0)
    return x


def last_row(x):
    return jnp.broadcast_to(x[7:8, :], x.shape)


def tendency(q, big, j):
    e = [east(q[f][j]) for f in range(4)]
    w = [west(q[f][j]) for f in range(4)]
    north = [q[f][j + 1] for f in range(4)]
    south = [q[f][j - 1] for f in range(4)]
    half_u, half_v = 0.5 * q[U][j], 0.5 * q[V][j]
    out = []
    for f in range(4):
        advect = half_u * (e[f] - w[f]) + half_v * (north[f] - south[f])
        lap = (e[f] + w[f]) + (north[f] + south[f]) - 4.0 * q[f][j]
        out.append((viscosity if f < 2 else diffusion) * lap - advect)
    press_x = 0.5 * (east(big[j]) - west(big[j]))
    press_y = 0.5 * (big[j + 1] - big[j - 1])
    out[U] = out[U] + coriolis * q[V][j] - press_x
    out[V] = out[V] - coriolis * q[U][j] - press_y
    return out


def ocean_steps(load, faces, carry, store, up, down, lane_mask):
    sub = lax.broadcasted_iota(jnp.int32, (8, LANES), 0)
    carry[...] = jnp.zeros_like(carry)

    def face(block, name, j, value):
        slot, first = FACES[name]
        faces[block, slot + j - first] = value

    def depth_sum(q, rows, base):
        big = {}
        for j in rows:
            b = (gravity_red * thermal) * q[T][j] - (gravity_red * haline) * q[S][j]
            big[j] = running_sum(b, sub) + carry[base + j]
            carry[base + j] = last_row(big[j])
        return big

    def body(block, _):
        q = [{}, {}, {}, {}]
        for f in (U, V):
            for j in range(-3, 7):
                q[f][j] = load(f, j, block)
        for f in (T, S):
            for j in range(-2, 6):
                q[f][j] = load(f, j, block)
        scale = 0.5 * time_step
        for j in range(-2, 6):
            speed = scale * (q[U][j] + east(q[U][j]))
            face(block, "up1", j, jnp.maximum(speed, 0.0))
            face(block, "um1", j, jnp.minimum(speed, 0.0))
        for j in range(-3, 6):
            speed = scale * (q[V][j] + q[V][j + 1])
            face(block, "vp1", j, jnp.maximum(speed, 0.0))
            face(block, "vm1", j, jnp.minimum(speed, 0.0))
        big = depth_sum(q, range(-2, 6), 2)
        one = [{}, {}, {}, {}]
        for j in range(-1, 5):
            rate = tendency(q, big, j)
            for f in range(4):
                value = q[f][j] + time_step * rate[f]
                if j < 0:
                    value = value * up
                if j > 3:
                    value = value * down
                if lane_mask is not None:
                    value = value * lane_mask
                one[f][j] = value
        for j in range(4):
            speed = scale * (one[U][j] + east(one[U][j]))
            face(block, "up2", j, jnp.maximum(speed, 0.0))
            face(block, "um2", j, jnp.minimum(speed, 0.0))
        for j in range(-1, 4):
            speed = scale * (one[V][j] + one[V][j + 1])
            face(block, "vp2", j, jnp.maximum(speed, 0.0))
            face(block, "vm2", j, jnp.minimum(speed, 0.0))
        big = depth_sum(one, range(-1, 5), 9)
        for j in range(4):
            rate = tendency(one, big, j)
            for f in range(4):
                store(f, j, block, 0.5 * (q[f][j] + one[f][j] + time_step * rate[f]))
        return 0

    lax.fori_loop(0, BLOCKS, body, 0)


def divergence(c, low, high, face):
    diff = {j: c[j + 1] - c[j] for j in range(low - 2, high + 1)}
    slope = {j: half_minmod(diff[j - 1], diff[j]) for j in range(low - 1, high + 1)}
    flux = {
        j: face("vp", j) * (c[j] + slope[j]) + face("vm", j) * (c[j + 1] - slope[j + 1])
        for j in range(low - 1, high)
    }
    out = {}
    for j in range(low, high):
        d = east(c[j]) - c[j]
        s = half_minmod(west(d), d)
        fx = face("up", j) * (c[j] + s) + face("um", j) * east(c[j] - s)
        out[j] = (fx - west(fx)) + (flux[j] - flux[j - 1])
    return out


def tracer_steps(load, faces, block, up, down, lane_mask):
    def face_of(stage):
        def get(name, j):
            slot, first = FACES[name + stage]
            return faces[block, slot + j - first]

        return get

    c = {j: load(j) for j in range(-4, 8)}
    change = divergence(c, -2, 6, face_of("1"))
    one = {}
    for j in range(-2, 6):
        value = c[j] - change[j]
        if j < 0:
            value = value * up
        if j > 3:
            value = value * down
        if lane_mask is not None:
            value = value * lane_mask
        one[j] = value.astype(jnp.bfloat16).astype(jnp.float32)
    change = divergence(one, 0, 4, face_of("2"))
    return [0.5 * (c[j] + one[j] - change[j]) for j in range(4)]


def place(j):
    return (j + 4) // 4, (j + 4) % 4


def edges_kernel(tr, tu, td, oc, ou, od, out):
    lane = lax.broadcasted_iota(jnp.int32, (LANES, LANES), 1)
    for tile, (tracer, ocean) in enumerate(((tu, ou), (tr, oc), (td, od))):
        acc = jnp.zeros((LANES, LANES), jnp.float32)
        for f in range(TRACERS + 4):
            x = tracer[f].astype(jnp.float32) if f < TRACERS else ocean[f - TRACERS]
            acc = jnp.where((lane >= 8 * f) & (lane < 8 * f + 8), roll(x, 8 * f + 4), acc)
        out[tile] = acc


def main_kernel(flags, tr, tu, td, oc, ou, od, two, ocean_two, strip, ocean_strip, faces, carry, cells):
    up, down = flags[0], flags[1]
    ocean = (ou, oc, od)

    def load(f, j, block):
        tile, y = place(j)
        return ocean[tile][f, rows_of(block, y), :]

    def store(f, j, block, value):
        ocean_two[f, j, pl.ds(block * 8, 8), :] = value

    ocean_steps(load, faces, carry, store, up, down, None)

    def body(t, _):
        for tile, ref in enumerate((tu, tr, td)):
            cells[tile] = ref[t].astype(jnp.float32)
        for block in range(BLOCKS):

            def cell(j):
                tile, y = place(j)
                return cells[tile, rows_of(block, y), :]

            result = tracer_steps(cell, faces, block, up, down, None)
            for j in range(4):
                two[t, j, block * 8 : block * 8 + 8, :] = result[j]
        return 0

    lax.fori_loop(0, TRACERS, body, 0)

    lane = lax.broadcasted_iota(jnp.int32, (LANES, LANES), 1)

    def own(x, base, acc):
        acc = jnp.where((lane >= base) & (lane < base + 8), roll(x, base + 8), acc)
        return jnp.where((lane >= base + 16) & (lane < base + 24), roll(x, base + 16), acc)

    for tile, (tracer, sea) in enumerate(((tu, ou), (tr, oc), (td, od))):
        for half in range(2):
            acc = jnp.zeros((LANES, LANES), jnp.float32)
            for k in range(COPIES):
                acc = own(tracer[half * COPIES + k].astype(jnp.float32), GROUP * k, acc)
            strip[half, tile] = acc
        for f in range(4):
            ocean_strip[f, tile] = own(sea[f], 0, jnp.zeros((LANES, LANES), jnp.float32))


def finish_kernel(
    flags, rates, wet_blocks, light, two, ocean_two, strip, ocean_strip, from_left, from_right,
    ocean_out, tracer_out, heating, faces, carry, cells, seas, strip_two, strip_ocean, reacted,
):
    up, down, left, right = (flags[k] for k in range(4))
    lane = lax.broadcasted_iota(jnp.int32, (LANES, LANES), 1)
    for tile in range(3):
        halo = jnp.where(lane % 8 < 4, roll(from_right[tile], -4), roll(from_left[tile], 4))

        def with_halo(f, base, x):
            return jnp.where((lane >= base + 8) & (lane < base + 16), roll(halo, base + 8 - 8 * f), x)

        for half in range(2):
            acc = strip[half, tile]
            for k in range(COPIES):
                acc = with_halo(half * COPIES + k, GROUP * k, acc)
            cells[half, tile] = acc
        for f in range(4):
            one = with_halo(TRACERS + f, 0, ocean_strip[f, tile])
            pair = one + roll(one, GROUP)
            seas[f, tile] = pair + roll(pair, 2 * GROUP) + roll(one, 4 * GROUP)
    place_in = lax.broadcasted_iota(jnp.int32, (8, LANES), 1) % GROUP
    lane_mask = jnp.where((place_in >= 8) & (place_in < 12), right, jnp.where((place_in >= 12) & (place_in < 16), left, 1.0))

    def load(f, j, block):
        tile, y = place(j)
        return seas[f, tile, rows_of(block, y), :]

    def store(f, j, block, value):
        strip_ocean[f, j, pl.ds(block * 8, 8), :] = value

    ocean_steps(load, faces, carry, store, up, down, lane_mask)

    def body(block, _):
        for half in range(2):

            def cell(j):
                tile, y = place(j)
                return cells[half, tile, rows_of(block, y), :]

            result = tracer_steps(cell, faces, block, up, down, lane_mask)
            for j in range(4):
                strip_two[half, j, pl.ds(block * 8, 8), :] = result[j]
        return 0

    lax.fori_loop(0, BLOCKS, body, 0)
    lanes = lax.broadcasted_iota(jnp.int32, (8, LANES), 1)
    sub = lax.broadcasted_iota(jnp.int32, (8, LANES), 0)
    wet = jnp.zeros((8, LANES), jnp.float32)
    for k in range(8):
        wet = jnp.where(lanes // 16 == k, wet_blocks[0, k].astype(jnp.float32), wet)
    half_wet = react_step * wet

    def patched(x, edge, base):
        x = jnp.where(lanes >= LANES - 4, roll(edge, 120 - base), x)
        return jnp.where(lanes < 4, roll(edge, -16 - base), x)

    def last(block, sums):
        sums = list(sums)
        at = pl.ds(block * 8, 8)
        for y in range(ROWS):
            edge = [strip_two[half, y, at, :] for half in range(2)]
            c = [patched(two[t, y, at, :], edge[t // COPIES], GROUP * (t % COPIES)) for t in range(TRACERS)]
            for a in range(TRACERS):
                total = rates[a, 0] * c[0]
                for b in range(1, TRACERS):
                    total = total + rates[a, b] * c[b]
                value = c[a] + half_wet * total
                reacted[a, rows_of(block, y), :] = value
                if a == 0:
                    att = water_atten + chloro_atten * value * value
            cum = running_sum(att, sub) + sums[y]
            sums[y] = last_row(cum)
            heat = wet * light[y : y + 1, :] * (jnp.exp(att - cum) - jnp.exp(-cum))
            heating[rows_of(block, y), :] = heat
            for f in range(4):
                value = patched(ocean_two[f, y, at, :], strip_ocean[f, y, at, :], 0)
                if f == T:
                    value = value + time_step * heat
                ocean_out[f, rows_of(block, y), :] = value
        return tuple(sums)

    zero = jnp.zeros((8, LANES), jnp.float32)
    lax.fori_loop(0, BLOCKS, last, (zero,) * ROWS)
    for a in range(TRACERS):
        tracer_out[a] = reacted[a].astype(jnp.bfloat16)


def vmem(count):
    return [pl.BlockSpec(memory_space=pltpu.VMEM)] * count


def smem(count):
    return [pl.BlockSpec(memory_space=pltpu.SMEM)] * count


def f32(*shape):
    return jax.ShapeDtypeStruct(shape, jnp.float32)


def limit(mib):
    return pltpu.CompilerParams(vmem_limit_bytes=mib << 20)


def cost(flops, size):
    return pl.CostEstimate(flops=flops, bytes_accessed=size, transcendentals=0)


STEP_SCRATCH = [
    pltpu.VMEM((BLOCKS, FACE_SLOTS, 8, LANES), jnp.float32),
    pltpu.VMEM((14, 8, LANES), jnp.float32),
]


def shards(ocean, tracers, wet_blocks, surface_light, rates):
    tr = tracers.reshape(TRACERS, LANES, LANES)
    oc = ocean.reshape(4, LANES, LANES)
    groups, tiles = lax.axis_size("grp"), lax.axis_size("tile")

    def shifted(x, axis, count):
        ahead = [(i, i + 1) for i in range(count - 1)]
        return lax.ppermute(x, axis, ahead), lax.ppermute(x, axis, [(j, i) for i, j in ahead])

    tu, td = shifted(tr, "grp", groups)
    ou, od = shifted(oc, "grp", groups)
    g, t = lax.axis_index("grp"), lax.axis_index("tile")
    flags = jnp.stack([g > 0, g < groups - 1, t > 0, t < tiles - 1]).astype(jnp.float32)
    fields = (tr, tu, td, oc, ou, od)
    edges = pl.pallas_call(
        edges_kernel, out_shape=f32(3, LANES, LANES), in_specs=vmem(6), out_specs=vmem(1)[0], compiler_params=limit(16), name="edges"
    )(*fields)
    from_left, from_right = shifted(edges, "tile", tiles)
    main = pl.pallas_call(
        main_kernel,
        out_shape=(
            f32(TRACERS, ROWS, LEVELS, LANES),
            f32(4, ROWS, LEVELS, LANES),
            f32(2, 3, LANES, LANES),
            f32(4, 3, LANES, LANES),
        ),
        in_specs=smem(1) + vmem(6),
        out_specs=vmem(4),
        scratch_shapes=STEP_SCRATCH + [pltpu.VMEM((3, LANES, LANES), jnp.float32)],
        cost_estimate=cost(40_000_000, 4_000_000),
        compiler_params=limit(16),
        name="main",
    )(flags, *fields)
    ocean_out, tracer_out, heating = pl.pallas_call(
        finish_kernel,
        out_shape=(
            f32(4, LANES, LANES),
            jax.ShapeDtypeStruct((TRACERS, LANES, LANES), jnp.bfloat16),
            f32(LANES, LANES),
        ),
        in_specs=smem(3) + vmem(7),
        out_specs=vmem(3),
        scratch_shapes=STEP_SCRATCH
        + [
            pltpu.VMEM((2, 3, LANES, LANES), jnp.float32),
            pltpu.VMEM((4, 3, LANES, LANES), jnp.float32),
            pltpu.VMEM((2, ROWS, LEVELS, LANES), jnp.float32),
            pltpu.VMEM((4, ROWS, LEVELS, LANES), jnp.float32),
            pltpu.VMEM((TRACERS, LANES, LANES), jnp.float32),
        ],
        compiler_params=limit(16),
        name="finish",
    )(flags, rates, wet_blocks, surface_light, *main, from_left, from_right)
    return (
        ocean_out.reshape(ocean.shape),
        tracer_out.reshape(tracers.shape),
        heating.reshape(LEVELS, ROWS, LANES),
    )


def solution(mesh):
    return jax.shard_map(
        shards,
        mesh=mesh,
        in_specs=(
            P(None, None, "grp", "tile"),
            P(None, None, "grp", "tile"),
            P("grp", "tile"),
            P("grp", "tile"),
            P(),
        ),
        out_specs=(
            P(None, None, "grp", "tile"),
            P(None, None, "grp", "tile"),
            P(None, "grp", "tile"),
        ),
        check_vma=False,
    )
```

time: 128 us -> 58.5 us (0.46)
  the two profiles are of different devices: /device:TPU:40 before, /device:TPU:54 now
where the time goes in v1:
time: 58.5 us; the launch traced here: 58.2 us
  starting transfers between devices  28.2 us (48%)
  Pallas kernels  17.1 us (29%)
  waiting for transfers between devices  9.5 us (16%)
  local copies, waits for them, and re-layouts  2.59 us (4%)
  between operations  0.76 us (1%)
    ppermute x3, starting transfers between devices, shifted(): lax.ppermute(x, axis, [(j, i) for i, j in ahead])  19.2 us
    ppermute x3, starting transfers between devices, shifted(): lax.ppermute(x, axis, ahead)  9.03 us
    pallas_call x1, Pallas kernels, shards(): pl.pallas_call(main_kernel, out_shape=(f32(TRACERS, ROWS, LEVELS, LANES),...  8.43 us
    pallas_call x1, Pallas kernels, shards(): pl.pallas_call(finish_kernel, out_shape=(f32(4, LANES, LANES), jax.ShapeD...  8.12 us
    ppermute x3, waiting for transfers between devices, shifted(): lax.ppermute(x, axis, ahead)  4.77 us
    ppermute x3, waiting for transfers between devices, shifted(): lax.ppermute(x, axis, [(j, i) for i, j in ahead])  4.73 us
    unnamed x14, local copies, waits for them, and re-layouts  2.59 us
  transfers between devices with their start and end apart: 6, of which 2 were waited for; matrix products, arithmetic and copies ran while one was open for 0% of the time, Pallas kernels for 14%

profile of v1, /device:TPU:54, one launch (start us, length us, event | category | flops | bytes accessed | tf_op | source)
XLA Modules:
  0.0 58.2 jit_solution(14443252904067633229)
XLA Ops:
  0.6 2.5 %collective-permute-start = (bf16[10,128,128]{2,1,0:T(8,128)(2,1)}, bf16[10,128,128]{2,1,0:T(8,128)(2,1)S(1)}, u32[]{:S(2)}, u32[]{:S(2)}) collective-permute-start(bf16[10,128,128]{2,1,0:T(8,128)(2,1)} %bitcast.9), channel_id=1, source_target_pairs={{0,96},{96,192},{192,288},{288,384},{384,480},{480,576},{576,672},... | collective-permute-start | bytes 983048 | tf_op jit(solution)/shard_map/ppermute | solution.py:379
  3.1 3.3 %collective-permute-start.1 = (bf16[10,128,128]{2,1,0:T(8,128)(2,1)}, bf16[10,128,128]{2,1,0:T(8,128)(2,1)S(1)}, u32[]{:S(2)}, u32[]{:S(2)}) collective-permute-start(bf16[10,128,128]{2,1,0:T(8,128)(2,1)} %bitcast.10), channel_id=1, source_target_pairs={{96,0},{192,96},{288,192},{384,288},{480,384},{576,480},{672,576},... | collective-permute-start | bytes 983048 | tf_op jit(solution)/shard_map/ppermute | solution.py:379
  6.5 4.6 %collective-permute-start.2 = (f32[4,128,128]{2,1,0:T(8,128)}, f32[4,128,128]{2,1,0:T(8,128)S(1)}, u32[]{:S(2)}, u32[]{:S(2)}) collective-permute-start(f32[4,128,128]{2,1,0:T(8,128)} %bitcast.13), channel_id=1, source_target_pairs={{0,96},{96,192},{192,288},{288,384},{384,480},{480,576},{576,672},... | collective-permute-start | bytes 786440 | tf_op jit(solution)/shard_map/ppermute | solution.py:379
  11.1 1.9 %collective-permute-start.3 = (f32[4,128,128]{2,1,0:T(8,128)}, f32[4,128,128]{2,1,0:T(8,128)S(1)}, u32[]{:S(2)}, u32[]{:S(2)}) collective-permute-start(f32[4,128,128]{2,1,0:T(8,128)} %bitcast.14), channel_id=1, source_target_pairs={{96,0},{192,96},{288,192},{384,288},{480,384},{576,480},{672,576},... | collective-permute-start | bytes 786440 | tf_op jit(solution)/shard_map/ppermute | solution.py:379
  13.0 4.8 %collective-permute-done.2.ou = f32[4,128,128]{2,1,0:T(8,128)S(1)} collective-permute-done((f32[4,128,128]{2,1,0:T(8,128)}, f32[4,128,128]{2,1,0:T(8,128)S(1)}, u32[]{:S(2)}, u32[]{:S(2)}) %collective-permute-start.2) | collective-permute-done | bytes 262176 | tf_op jit(solution)/shard_map/ppermute | solution.py:379
  17.8 4.7 %collective-permute-done.3.od = f32[4,128,128]{2,1,0:T(8,128)S(1)} collective-permute-done((f32[4,128,128]{2,1,0:T(8,128)}, f32[4,128,128]{2,1,0:T(8,128)S(1)}, u32[]{:S(2)}, u32[]{:S(2)}) %collective-permute-start.3) | collective-permute-done | bytes 262176 | tf_op jit(solution)/shard_map/ppermute | solution.py:379
  22.5 0.0 collective-permute-done.tu
  22.5 0.0 collective-permute-done.1.td
  22.5 1.0 %copy-done = bf16[10,32,4,128]{3,2,1,0:T(4,128)(2,1)S(1)} copy-done((bf16[10,32,4,128]{3,2,1,0:T(4,128)(2,1)S(1)}, bf16[10,32,4,128]{3,2,1,0:T(4,128)(2,1)}, u32[]{:S(2)}) %copy-start) | copy-done | bytes 327704
  23.5 0.9 %copy-done.2 = f32[4,32,4,128]{3,2,1,0:T(4,128)S(1)} copy-done((f32[4,32,4,128]{3,2,1,0:T(4,128)S(1)}, f32[4,32,4,128]{3,2,1,0:T(4,128)}, u32[]{:S(2)}) %copy-start.2) | copy-done | bytes 262168
  24.5 0.5 edges.1
  25.0 1.9 %collective-permute-start.4 = (f32[3,128,128]{2,1,0:T(8,128)S(1)}, f32[3,128,128]{2,1,0:T(8,128)S(1)}, u32[]{:S(2)}, u32[]{:S(2)}) collective-permute-start(f32[3,128,128]{2,1,0:T(8,128)S(1)} %edges.1), channel_id=1, source_target_pairs={{0,1},{1,2},{2,3},{3,4},{4,5},{5,6},{6,7},{7,8},{8,9},{9,10},{10,1... | collective-permute-start | bytes 589832 | tf_op jit(solution)/shard_map/ppermute | solution.py:379
  26.9 13.9 %collective-permute-start.5 = (f32[3,128,128]{2,1,0:T(8,128)S(1)}, f32[3,128,128]{2,1,0:T(8,128)S(1)}, u32[]{:S(2)}, u32[]{:S(2)}) collective-permute-start(f32[3,128,128]{2,1,0:T(8,128)S(1)} %edges.1), channel_id=1, source_target_pairs={{1,0},{2,1},{3,2},{4,3},{5,4},{6,5},{7,6},{8,7},{9,8},{10,9},{11,1... | collective-permute-start | bytes 589832 | tf_op jit(solution)/shard_map/ppermute | solution.py:379
  40.8 0.1 add_convert_fusion.flags
  40.9 0.0 copy-done.1
  40.9 0.0 copy-done.3
  40.9 8.4 %main.1 = (f32[10,4,32,128]{3,2,1,0:T(8,128)S(1)}, f32[4,4,32,128]{3,2,1,0:T(8,128)S(1)}, f32[2,3,128,128]{3,2,1,0:T(8,128)S(1)}, f32[4,3,128,128]{3,2,1,0:T(8,128)S(1)}) custom-call(f32[4]{0:T(128)S(1)} %add_convert_fusion.flags, bf16[10,128,128]{2,1,0:T(8,128)(2,1)S(1)} %bitcast.12, bf16[10,128,128]{2,1,0:T(8,128)(2,1)S(1)} %collective-permute-done.tu, ...), custom_call_target="tpu_custom_call" | custom-call | flops 40000000 | bytes 4000000 | tf_op jit(solution)/shard_map/main/pallas_call | solution.py:390
  49.4 0.0 collective-permute-done.4.from_left
  49.4 0.0 collective-permute-done.5.from_right
  49.4 0.0 copy-start.5
  49.4 0.0 copy-start.6
  49.4 0.0 copy-done.4
  49.4 0.7 %copy-done.5 = f32[4,128]{1,0:T(4,128)S(1)} copy-done((f32[4,128]{1,0:T(4,128)S(1)}, f32[4,128]{1,0:T(4,128)}, u32[]{:S(2)}) %copy-start.5) | copy-done | bytes 2072
  50.1 8.1 %finish.1 = (f32[4,128,128]{2,1,0:T(8,128)}, bf16[10,128,128]{2,1,0:T(8,128)(2,1)}, f32[128,128]{1,0:T(8,128)}) custom-call(f32[4]{0:T(128)S(1)} %add_convert_fusion.flags, f32[10,10]{1,0:T(8,128)S(1)} %copy-done.4, s32[1,8]{1,0:T(1,128)S(1)} %copy-done.6, f32[4,128]{1,0:T(4,128)S(1)} %copy-done.5, f32[10,4,32,128]{3,2,1,0:T(8,128)S(1)} %get-tuple-element.10.two, ...), custom_call_target="tpu_custom_call" | custom-call | tf_op jit(solution)/shard_map/finish/pallas_call | solution.py:405
  (6 shorter events, 0.0 us)
Async XLA Ops:
  0.6 21.9 %collective-permute-start = (bf16[10,128,128]{2,1,0:T(8,128)(2,1)}, bf16[10,128,128]{2,1,0:T(8,128)(2,1)S(1)}, u32[]{:S(2)}, u32[]{:S(2)}) collective-permute-start(bf16[10,128,128]{2,1,0:T(8,128)(2,1)} %bitcast.9), channel_id=1, source_target_pairs={{0,96},{96,192},{192,288},{288,384},{384,480},{480,576},{576,672},... | collective-permute-start | bytes 983048 | tf_op jit(solution)/shard_map/ppermute | solution.py:379
  3.1 19.4 %collective-permute-start.1 = (bf16[10,128,128]{2,1,0:T(8,128)(2,1)}, bf16[10,128,128]{2,1,0:T(8,128)(2,1)S(1)}, u32[]{:S(2)}, u32[]{:S(2)}) collective-permute-start(bf16[10,128,128]{2,1,0:T(8,128)(2,1)} %bitcast.10), channel_id=1, source_target_pairs={{96,0},{192,96},{288,192},{384,288},{480,384},{576,480},{672,576},... | collective-permute-start | bytes 983048 | tf_op jit(solution)/shard_map/ppermute | solution.py:379
  6.5 11.3 %collective-permute-start.2 = (f32[4,128,128]{2,1,0:T(8,128)}, f32[4,128,128]{2,1,0:T(8,128)S(1)}, u32[]{:S(2)}, u32[]{:S(2)}) collective-permute-start(f32[4,128,128]{2,1,0:T(8,128)} %bitcast.13), channel_id=1, source_target_pairs={{0,96},{96,192},{192,288},{288,384},{384,480},{480,576},{576,672},... | collective-permute-start | bytes 786440 | tf_op jit(solution)/shard_map/ppermute | solution.py:379
  11.1 11.4 %collective-permute-start.3 = (f32[4,128,128]{2,1,0:T(8,128)}, f32[4,128,128]{2,1,0:T(8,128)S(1)}, u32[]{:S(2)}, u32[]{:S(2)}) collective-permute-start(f32[4,128,128]{2,1,0:T(8,128)} %bitcast.14), channel_id=1, source_target_pairs={{96,0},{192,96},{288,192},{384,288},{480,384},{576,480},{672,576},... | collective-permute-start | bytes 786440 | tf_op jit(solution)/shard_map/ppermute | solution.py:379
  22.5 1.0 %copy-start = (bf16[10,32,4,128]{3,2,1,0:T(4,128)(2,1)S(1)}, bf16[10,32,4,128]{3,2,1,0:T(4,128)(2,1)}, u32[]{:S(2)}) copy-start(bf16[10,32,4,128]{3,2,1,0:T(4,128)(2,1)} %param.6) | copy-start | bytes 983044
  23.5 0.9 %copy-start.2 = (f32[4,32,4,128]{3,2,1,0:T(4,128)S(1)}, f32[4,32,4,128]{3,2,1,0:T(4,128)}, u32[]{:S(2)}) copy-start(f32[4,32,4,128]{3,2,1,0:T(4,128)} %param.5) | copy-start | bytes 786436
  24.5 16.5 %copy-start.1 = (bf16[10,32,4,128]{3,2,1,0:T(4,128)(2,1)S(1)}, bf16[10,32,4,128]{3,2,1,0:T(4,128)(2,1)}, u32[]{:S(2)}) copy-start(bf16[10,32,4,128]{3,2,1,0:T(4,128)(2,1)} %param.6) | copy-start | bytes 983044
  24.5 16.5 %copy-start.3 = (f32[4,32,4,128]{3,2,1,0:T(4,128)S(1)}, f32[4,32,4,128]{3,2,1,0:T(4,128)}, u32[]{:S(2)}) copy-start(f32[4,32,4,128]{3,2,1,0:T(4,128)} %param.5) | copy-start | bytes 786436
  25.0 24.4 %collective-permute-start.4 = (f32[3,128,128]{2,1,0:T(8,128)S(1)}, f32[3,128,128]{2,1,0:T(8,128)S(1)}, u32[]{:S(2)}, u32[]{:S(2)}) collective-permute-start(f32[3,128,128]{2,1,0:T(8,128)S(1)} %edges.1), channel_id=1, source_target_pairs={{0,1},{1,2},{2,3},{3,4},{4,5},{5,6},{6,7},{7,8},{8,9},{9,10},{10,1... | collective-permute-start | bytes 589832 | tf_op jit(solution)/shard_map/ppermute | solution.py:379
  26.9 22.5 %collective-permute-start.5 = (f32[3,128,128]{2,1,0:T(8,128)S(1)}, f32[3,128,128]{2,1,0:T(8,128)S(1)}, u32[]{:S(2)}, u32[]{:S(2)}) collective-permute-start(f32[3,128,128]{2,1,0:T(8,128)S(1)} %edges.1), channel_id=1, source_target_pairs={{1,0},{2,1},{3,2},{4,3},{5,4},{6,5},{7,6},{8,7},{9,8},{10,9},{11,1... | collective-permute-start | bytes 589832 | tf_op jit(solution)/shard_map/ppermute | solution.py:379
  40.9 8.5 %copy-start.4 = (f32[10,10]{1,0:T(8,128)S(1)}, f32[10,10]{1,0:T(8,128)}, u32[]{:S(2)}) copy-start(f32[10,10]{1,0:T(8,128)} %rates.1) | copy-start | bytes 1204
  49.4 0.7 %copy-start.5 = (f32[4,128]{1,0:T(4,128)S(1)}, f32[4,128]{1,0:T(4,128)}, u32[]{:S(2)}) copy-start(f32[4,128]{1,0:T(4,128)} %light.1) | copy-start | bytes 6148
  49.4 0.7 %copy-start.6 = (s32[1,8]{1,0:T(1,128)S(1)}, s32[1,8]{1,0:T(1,128)}, u32[]{:S(2)}) copy-start(s32[1,8]{1,0:T(1,128)} %wet_blocks.1) | copy-start | bytes 100

commit v2 on v1

v2 whole, which is shorter than its diff:
```python
import jax
import jax.numpy as jnp
from jax import lax
from jax.experimental import pallas as pl
from jax.experimental.pallas import tpu as pltpu
from jax.sharding import PartitionSpec as P

LEVELS = 32
ROWS = 4
LANES = 128
BLOCKS = LEVELS // 8
GROUP = 24
COPIES = 5
TRACERS = 10

time_step = 0.3
coriolis = 0.2
viscosity = 0.1
diffusion = 0.05
thermal = 0.2
haline = 0.15
gravity_red = 0.05
react_step = 0.5
water_atten = 0.3
chloro_atten = 0.2

U, V, T, S = range(4)
FACES = {}
_count = 0
for _name, _first, _number in (
    ("up1", -2, 8),
    ("um1", -2, 8),
    ("vp1", -3, 9),
    ("vm1", -3, 9),
    ("up2", 0, 4),
    ("um2", 0, 4),
    ("vp2", -1, 5),
    ("vm2", -1, 5),
):
    FACES[_name] = (_count, _first)
    _count += _number
FACE_SLOTS = _count
HALO_BEFORE = [(f, j) for f in (U, V) for j in (-3, -2, -1)] + [(f, j) for f in (T, S) for j in (-2, -1)]
HALO_AFTER = [(f, j) for f in (U, V) for j in (4, 5, 6)] + [(f, j) for f in (T, S) for j in (4, 5)]
HALO = {key: k for k, key in enumerate(HALO_BEFORE + HALO_AFTER)}
STRIP = {key: k for k, key in enumerate([(f, j) for f in (U, V) for j in range(-3, 7)] + [(f, j) for f in (T, S) for j in range(-2, 6)])}
PARTS = 2 * len(HALO_BEFORE)


def roll(x, shift, axis=1):
    return pltpu.roll(x, shift % x.shape[axis], axis)


def east(x):
    return roll(x, -1)


def west(x):
    return roll(x, 1)


def minmod(a, b):
    return jnp.maximum(jnp.minimum(a, b), jnp.minimum(jnp.maximum(a, b), 0.0))


def rows_of(block, y):
    return pl.ds(block * 8 * ROWS + y, 8, stride=ROWS)


def running_sum(x, sub):
    for step in (1, 2, 4):
        x = x + jnp.where(sub >= step, roll(x, step, 0), 0.0)
    return x


def last_row(x):
    return jnp.broadcast_to(x[7:8, :], x.shape)


def tendency(q, big, j):
    e = [east(q[f][j]) for f in range(4)]
    w = [west(q[f][j]) for f in range(4)]
    north = [q[f][j + 1] for f in range(4)]
    south = [q[f][j - 1] for f in range(4)]
    half_u, half_v = 0.5 * q[U][j], 0.5 * q[V][j]
    out = []
    for f in range(4):
        advect = half_u * (e[f] - w[f]) + half_v * (north[f] - south[f])
        lap = (e[f] + w[f]) + (north[f] + south[f]) - 4.0 * q[f][j]
        out.append((viscosity if f < 2 else diffusion) * lap - advect)
    press_x = 0.5 * (east(big[j]) - west(big[j]))
    press_y = 0.5 * (big[j + 1] - big[j - 1])
    out[U] = out[U] + coriolis * q[V][j] - press_x
    out[V] = out[V] - coriolis * q[U][j] - press_y
    return out


def ocean_steps(load, faces, carry, store, up, down, lane_mask, spread):
    sub = lax.broadcasted_iota(jnp.int32, (8, LANES), 0)
    carry[...] = jnp.zeros_like(carry)
    scale = 0.25 * time_step

    def body(block, _):
        at = pl.ds(block * 8, 8)

        def speeds(stage, axis, j, a, b):
            speed = spread(scale * (a + b))
            for sign, part in (("p", jnp.maximum), ("m", jnp.minimum)):
                slot, first = FACES[axis + sign + stage]
                faces[slot + j - first, at, :] = part(speed, 0.0)

        def depth_sum(q, rows, base):
            big = {}
            for j in rows:
                b = (gravity_red * thermal) * q[T][j] - (gravity_red * haline) * q[S][j]
                big[j] = running_sum(b, sub) + carry[base + j]
                carry[base + j] = last_row(big[j])
            return big

        q = [{}, {}, {}, {}]
        for f, j in STRIP:
            q[f][j] = load(f, j, at)
        for j in range(-2, 6):
            speeds("1", "u", j, q[U][j], east(q[U][j]))
        for j in range(-3, 6):
            speeds("1", "v", j, q[V][j], q[V][j + 1])
        big = depth_sum(q, range(-2, 6), 2)
        one = [{}, {}, {}, {}]
        for j in range(-1, 5):
            rate = tendency(q, big, j)
            for f in range(4):
                value = q[f][j] + time_step * rate[f]
                if j < 0:
                    value = value * up
                if j > 3:
                    value = value * down
                if lane_mask is not None:
                    value = value * lane_mask
                one[f][j] = value
        for j in range(4):
            speeds("2", "u", j, one[U][j], east(one[U][j]))
        for j in range(-1, 4):
            speeds("2", "v", j, one[V][j], one[V][j + 1])
        big = depth_sum(one, range(-1, 5), 9)
        for j in range(4):
            rate = tendency(one, big, j)
            for f in range(4):
                store(f, j, at, 0.5 * (q[f][j] + one[f][j] + time_step * rate[f]))
        return 0

    lax.fori_loop(0, BLOCKS, body, 0)


def advance(c, low, high, face, finish):
    diff_before = c(low - 1) - c(low - 2)
    left_before = flux_before = None
    for j in range(low - 1, high + 1):
        here = c(j)
        diff = c(j + 1) - here
        slope = minmod(diff_before, diff)
        twice = here + here
        flux = None
        if left_before is not None:
            flux = face("vp", j - 1) * left_before + face("vm", j - 1) * (twice - slope)
        if flux_before is not None:
            cell = c(j - 1)
            plus, minus, further = east(cell), west(cell), roll(cell, -2)
            d = plus - cell
            s = minmod(cell - minus, d)
            right = (plus + plus) - minmod(d, further - plus)
            fx = face("up", j - 1) * ((cell + cell) + s) + face("um", j - 1) * right
            finish(j - 1, (fx - west(fx)) + (flux - flux_before))
        diff_before, left_before, flux_before = diff, twice + slope, flux


def tracer_steps(load, faces, at, up, down, lane_mask, store):
    def face_of(stage):
        def get(name, j):
            slot, first = FACES[name + stage]
            return faces[slot + j - first, at, :]

        return get

    cells, one = {}, {}

    def cell(j):
        if j not in cells:
            cells[j] = load(j)
        return cells[j]

    def first(j, change):
        value = cell(j) - change
        if j == -1:
            value = value * up
        if j == ROWS:
            value = value * down
        if lane_mask is not None:
            value = value * lane_mask
        one[j] = value.astype(jnp.bfloat16).astype(jnp.float32)

    def second(j, change):
        store(j, 0.5 * ((cell(j) + one[j]) - change))

    advance(cell, -2, ROWS + 2, face_of("1"), first)
    advance(lambda j: one[j], 0, ROWS, face_of("2"), second)


def whole_iota(axis):
    return lax.broadcasted_iota(jnp.int32, (LANES, LANES), axis)


def one_hot(where):
    return jnp.where(where, 1.0, 0.0).astype(jnp.bfloat16)


def level_rows(y):
    return slice(y * LEVELS, (y + 1) * LEVELS)


def pack_kernel(tr, oc, to_next, to_previous, own_ocean, edges, tracer_in, ocean_in, sems):
    half = pl.ds(0, COPIES), pl.ds(COPIES, COPIES)
    copies = [pltpu.make_async_copy(tr.at[half[k]], tracer_in.at[half[k]], sems.at[k]) for k in range(2)]
    copies.append(pltpu.make_async_copy(oc, ocean_in, sems.at[2]))
    for copy in copies:
        copy.start()
    row, lane = whole_iota(0), whole_iota(1)
    reorder = one_hot(lane == (row % LEVELS) * ROWS + row // LEVELS)
    acc = jnp.zeros((LANES, LANES), jnp.float32)

    def with_edges(acc, x, base):
        acc = jnp.where((lane >= base) & (lane < base + 4), roll(x, base), acc)
        return jnp.where((lane >= base + 4) & (lane < base + 8), roll(x, base + 8), acc)

    for k in range(TRACERS):
        if k % COPIES == 0:
            copies[k // COPIES].wait()
        x = jnp.dot(reorder, tracer_in[k], preferred_element_type=jnp.float32)
        narrow = x.astype(jnp.bfloat16)
        to_next[k * LANES : (k + 1) * LANES, :] = narrow
        to_previous[k * LANES : (k + 1) * LANES, :] = narrow
        acc = with_edges(acc, x, GROUP * (k % COPIES) + 8 + 8 * (k // COPIES))
    base = TRACERS * LANES
    copies[2].wait()
    for f in range(4):
        levels = []
        for y in range(ROWS):
            x = ocean_in[f, pl.ds(y, LEVELS, stride=ROWS), :]
            own_ocean[f, level_rows(y), :] = x
            high = x.astype(jnp.bfloat16)
            low = (x - high.astype(jnp.float32)).astype(jnp.bfloat16)
            levels.append((high, low))
        acc = with_edges(acc, own_ocean[f], GROUP * f)
        wanted = ((1, 2, 3), (0, 1, 2)) if f in (U, V) else ((2, 3), (0, 1))
        parts = [[part for y in rows for part in levels[y]] for rows in wanted]
        for out, side in zip((to_next, to_previous), parts):
            for k, part in enumerate(side):
                out[base + k * LEVELS : base + (k + 1) * LEVELS, :] = part
        base += len(parts[0]) * LEVELS
    edges[...] = acc


def main_kernel(flags, mine, before, after, own_ocean, two, ocean_two, strip, ocean_strip, faces, carry, halo):
    up, down = flags[0], flags[1]
    sides = (before, mine, after)
    for side, names in ((before, HALO_BEFORE), (after, HALO_AFTER)):

        def part(k):
            at = TRACERS * LANES + k * LEVELS
            return side[at : at + LEVELS, :].astype(jnp.float32)

        for k, key in enumerate(names):
            halo[HALO[key]] = part(2 * k) + part(2 * k + 1)

    def load(f, j, at):
        if 0 <= j < ROWS:
            return own_ocean[f, pl.ds(at.start + j * LEVELS, 8), :]
        return halo[HALO[f, j], at, :]

    def store(f, j, at, value):
        ocean_two[f, j, at, :] = value

    ocean_steps(load, faces, carry, store, up, down, None, lambda x: x)

    def body(t, _):
        for part in range(LEVELS // 16):
            for half in range(2):

                def cell(j):
                    y = (j + 4) % 4
                    at = pl.multiple_of(t * LANES + y * LEVELS + part * 16, 16)
                    return sides[(j + 4) // 4][pl.ds(at, 16), :].astype(jnp.float32)[half * 8 : half * 8 + 8]

                at = slice(part * 16 + half * 8, part * 16 + half * 8 + 8)

                def put(j, value):
                    two[t, j, at, :] = value

                tracer_steps(cell, faces, at, up, down, None, put)
        return 0

    lax.fori_loop(0, TRACERS, body, 0)

    row, lane = whole_iota(0), whole_iota(1)
    source = jnp.where(row >= LANES - 8, row - (LANES - 8), jnp.where(row < 8, row + 16, -LANES * 4))
    picks = [one_hot(lane == source + GROUP * k) for k in range(COPIES)]
    for tile in range(3):
        for half in range(2):
            acc = None
            for k in range(COPIES):
                at = (half * COPIES + k) * LANES
                term = jnp.dot(sides[tile][at : at + LANES, :], picks[k], preferred_element_type=jnp.float32)
                acc = term if acc is None else acc + term
            strip[half, tile] = acc
    lanes = lax.broadcasted_iota(jnp.int32, (LEVELS, LANES), 1)
    for (f, j), k in STRIP.items():
        x = own_ocean[f, level_rows(j), :] if 0 <= j < ROWS else halo[HALO[f, j]]
        x = jnp.where(lanes < 8, roll(x, 8), roll(x, 16))
        ocean_strip[k] = jnp.where((lanes < 8) | ((lanes >= 16) & (lanes < 24)), x, 0.0)


def finish_kernel(
    flags, two, ocean_two, strip, ocean_strip, halo, halo_before, halo_after, rates_in, wet_in, light_in,
    ocean_out, tracer_out, heating, faces, carry, cells, strip_two, strip_ocean, reacted, narrow, ocean_done, heat_done,
    rates, wet_blocks, light, sems,
):
    small = [
        pltpu.make_async_copy(source, target, sems.at[k])
        for k, (source, target) in enumerate(((rates_in, rates), (wet_in, wet_blocks), (light_in, light)))
    ]
    for copy in small:
        copy.start()
    up, down, left, right = (flags[k] for k in range(4))
    lanes = lax.broadcasted_iota(jnp.int32, (LEVELS, LANES), 1)

    def halo_row(j):
        if j < 0:
            return halo_before[level_rows(j + 2), :]
        if j < ROWS:
            return halo[level_rows(j), :]
        return halo_after[level_rows(j - ROWS), :]

    middle = (lanes % GROUP >= 8) & (lanes % GROUP < 16)
    for j in range(-4, 8):
        tile, y = (j + 4) // 4, (j + 4) % 4
        for half in range(2):
            x = strip[half, tile, level_rows(y), :]
            if -2 <= j < 6:
                fresh = halo_row(j)
                x = jnp.where(middle, roll(fresh, -8) if half else fresh, x)
            cells[half, j + 4] = x

    place_in = lax.broadcasted_iota(jnp.int32, (8, LANES), 1)
    first_group = place_in < GROUP
    first_middle = (place_in >= 8) & (place_in < 16)
    place_in = place_in % GROUP
    lane_mask = jnp.where((place_in >= 8) & (place_in < 12), right, jnp.where((place_in >= 12) & (place_in < 16), left, 1.0))

    def load(f, j, at):
        x = ocean_strip[STRIP[f, j], at, :]
        if -2 <= j < 6:
            if j < 0:
                fresh = halo_before[pl.ds(at.start + (j + 2) * LEVELS, 8), :]
            elif j < ROWS:
                fresh = halo[pl.ds(at.start + j * LEVELS, 8), :]
            else:
                fresh = halo_after[pl.ds(at.start + (j - ROWS) * LEVELS, 8), :]
            x = jnp.where(first_middle, roll(fresh, 8 - GROUP * f), x)
        return x

    def store(f, j, at, value):
        strip_ocean[f, j, at, :] = value

    def spread(x):
        x = jnp.where(first_group, x, 0.0)
        pair = x + roll(x, GROUP)
        return pair + roll(pair, 2 * GROUP) + roll(x, 4 * GROUP)

    ocean_steps(load, faces, carry, store, up, down, lane_mask, spread)

    def body(block, _):
        at = pl.ds(block * 8, 8)
        for half in range(2):

            def put(j, value):
                strip_two[half, j, at, :] = value

            tracer_steps(lambda j: cells[half, j + 4, at, :], faces, at, up, down, lane_mask, put)
        return 0

    lax.fori_loop(0, BLOCKS, body, 0)
    for copy in small:
        copy.wait()
    lane = lax.broadcasted_iota(jnp.int32, (8, LANES), 1)
    sub = lax.broadcasted_iota(jnp.int32, (8, LANES), 0)
    wet = jnp.zeros((8, LANES), jnp.float32)
    for k in range(8):
        wet = jnp.where(lane // 16 == k, wet_blocks[0, k].astype(jnp.float32), wet)
    half_wet = react_step * wet

    def patched(x, edge, base):
        x = jnp.where(lane >= LANES - 4, roll(edge, 120 - base), x)
        return jnp.where(lane < 4, roll(edge, -16 - base), x)

    def results(block):
        rows = pl.ds(pl.multiple_of(block * 8 * ROWS, 8 * ROWS), 8 * ROWS)
        return (
            pltpu.make_async_copy(narrow.at[:, rows, :], tracer_out.at[:, rows, :], sems.at[3 + block]),
            pltpu.make_async_copy(ocean_done.at[:, rows, :], ocean_out.at[:, rows, :], sems.at[3 + BLOCKS + block]),
            pltpu.make_async_copy(heat_done.at[rows, :], heating.at[rows, :], sems.at[3 + 2 * BLOCKS + block]),
        )

    def last(block, sums):
        sums = list(sums)
        at = pl.ds(block * 8, 8)
        for pair in range(0, ROWS, 2):
            ys = (pair, pair + 1)
            edge = {y: [strip_two[half, y, at, :] for half in range(2)] for y in ys}
            c = {
                y: [patched(two[t, y, at, :], edge[y][t // COPIES], GROUP * (t % COPIES)) for t in range(TRACERS)]
                for y in ys
            }
            att = {}
            for a in range(TRACERS):
                total = {}
                for b in range(TRACERS):
                    rate = rates[a, b]
                    for y in ys:
                        term = rate * c[y][b]
                        total[y] = term if b == 0 else total[y] + term
                for y in ys:
                    value = c[y][a] + half_wet * total[y]
                    reacted[a, rows_of(block, y), :] = value
                    if a == 0:
                        att[y] = water_atten + chloro_atten * value * value
            for y in ys:
                cum = running_sum(att[y], sub) + sums[y]
                sums[y] = last_row(cum)
                heat = wet * light[y : y + 1, :] * (jnp.exp(att[y] - cum) - jnp.exp(-cum))
                heat_done[rows_of(block, y), :] = heat
                for f in range(4):
                    value = patched(ocean_two[f, y, at, :], strip_ocean[f, y, at, :], 0)
                    if f == T:
                        value = value + time_step * heat
                    ocean_done[f, rows_of(block, y), :] = value
        rows = pl.ds(pl.multiple_of(block * 8 * ROWS, 8 * ROWS), 8 * ROWS)
        narrow[:, rows, :] = reacted[:, rows, :].astype(jnp.bfloat16)
        for copy in results(block):
            copy.start()
        return tuple(sums)

    zero = jnp.zeros((8, LANES), jnp.float32)
    lax.fori_loop(0, BLOCKS, last, (zero,) * ROWS)
    for block in range(BLOCKS):
        for copy in results(block):
            copy.wait()


def vmem(count):
    return [pl.BlockSpec(memory_space=pltpu.VMEM)] * count


def smem(count):
    return [pl.BlockSpec(memory_space=pltpu.SMEM)] * count


def hbm(count):
    return [pl.BlockSpec(memory_space=pltpu.HBM)] * count


def in_hbm(x):
    return pltpu.with_memory_space_constraint(x, pltpu.HBM)


def f32(*shape):
    return jax.ShapeDtypeStruct(shape, jnp.float32)


def bf16(*shape):
    return jax.ShapeDtypeStruct(shape, jnp.bfloat16)


def limit(mib):
    return pltpu.CompilerParams(vmem_limit_bytes=mib << 20)


def cost(flops, size):
    return pl.CostEstimate(flops=flops, bytes_accessed=size, transcendentals=0)


STEP_SCRATCH = [
    pltpu.VMEM((FACE_SLOTS, LEVELS, LANES), jnp.float32),
    pltpu.VMEM((14, 8, LANES), jnp.float32),
]


def pack(tr, oc):
    payload = TRACERS * LANES + PARTS * LEVELS
    return pl.pallas_call(
        pack_kernel,
        out_shape=(bf16(payload, LANES), bf16(payload, LANES), f32(4, LANES, LANES), f32(LANES, LANES)),
        in_specs=hbm(2),
        out_specs=vmem(4),
        scratch_shapes=[
            pltpu.VMEM((TRACERS, LANES, LANES), jnp.bfloat16),
            pltpu.VMEM((4, LANES, LANES), jnp.float32),
            pltpu.SemaphoreType.DMA((3,)),
        ],
        compiler_params=limit(8),
        name="pack",
    )(in_hbm(tr), in_hbm(oc))


def transport(flags, mine, before, after, own_ocean):
    return pl.pallas_call(
        main_kernel,
        out_shape=(
            f32(TRACERS, ROWS, LEVELS, LANES),
            f32(4, ROWS, LEVELS, LANES),
            f32(2, 3, LANES, LANES),
            f32(len(STRIP), LEVELS, LANES),
        ),
        in_specs=smem(1) + vmem(4),
        out_specs=vmem(4),
        scratch_shapes=STEP_SCRATCH + [pltpu.VMEM((len(HALO), LEVELS, LANES), jnp.float32)],
        cost_estimate=cost(40_000_000, 4_000_000),
        compiler_params=limit(8),
        name="main",
    )(flags, mine, before, after, own_ocean)


def finish(flags, main, halos, rates, wet_blocks, surface_light):
    return pl.pallas_call(
        finish_kernel,
        out_shape=(f32(4, LANES, LANES), bf16(TRACERS, LANES, LANES), f32(LANES, LANES)),
        in_specs=smem(1) + vmem(7) + hbm(3),
        out_specs=hbm(3),
        scratch_shapes=STEP_SCRATCH
        + [
            pltpu.VMEM((2, 12, LEVELS, LANES), jnp.float32),
            pltpu.VMEM((2, ROWS, LEVELS, LANES), jnp.float32),
            pltpu.VMEM((4, ROWS, LEVELS, LANES), jnp.float32),
            pltpu.VMEM((TRACERS, LANES, LANES), jnp.float32),
            pltpu.VMEM((TRACERS, LANES, LANES), jnp.bfloat16),
            pltpu.VMEM((4, LANES, LANES), jnp.float32),
            pltpu.VMEM((LANES, LANES), jnp.float32),
            pltpu.SMEM(rates.shape, jnp.float32),
            pltpu.SMEM(wet_blocks.shape, jnp.int32),
            pltpu.VMEM(surface_light.shape, jnp.float32),
            pltpu.SemaphoreType.DMA((3 + 3 * BLOCKS,)),
        ],
        compiler_params=limit(12),
        name="finish",
    )(flags, *main, *halos, *map(in_hbm, (rates, wet_blocks, surface_light)))


def shards(ocean, tracers, wet_blocks, surface_light, rates):
    tr = tracers.reshape(TRACERS, LANES, LANES)
    oc = ocean.reshape(4, LANES, LANES)
    groups, tiles = lax.axis_size("grp"), lax.axis_size("tile")

    def ahead(x, axis, count):
        return lax.ppermute(x, axis, [(i, i + 1) for i in range(count - 1)])

    def back(x, axis, count):
        return lax.ppermute(x, axis, [(i + 1, i) for i in range(count - 1)])

    g, t = lax.axis_index("grp"), lax.axis_index("tile")
    flags = jnp.stack([g > 0, g < groups - 1, t > 0, t < tiles - 1]).astype(jnp.float32)
    to_next, to_previous, own_ocean, edges = pack(tr, oc)
    from_left = ahead(edges, "tile", tiles)
    before = ahead(to_next, "grp", groups)
    after = back(to_previous, "grp", groups)
    from_right = back(edges, "tile", tiles)
    lane = lax.broadcasted_iota(jnp.int32, (LANES, LANES), 1)
    halo = jnp.where(lane % 8 < 4, from_right, from_left)
    halo_before = ahead(halo[2 * LEVELS :], "grp", groups)
    halo_after = back(halo[: 2 * LEVELS], "grp", groups)
    main = transport(flags, to_next, before, after, own_ocean)
    ocean_out, tracer_out, heating = finish(
        flags, main, (halo, halo_before, halo_after), rates, wet_blocks, surface_light
    )
    return (
        ocean_out.reshape(ocean.shape),
        tracer_out.reshape(tracers.shape),
        heating.reshape(LEVELS, ROWS, LANES),
    )


def solution(mesh):
    return jax.shard_map(
        shards,
        mesh=mesh,
        in_specs=(
            P(None, None, "grp", "tile"),
            P(None, None, "grp", "tile"),
            P("grp", "tile"),
            P("grp", "tile"),
            P(),
        ),
        out_specs=(
            P(None, None, "grp", "tile"),
            P(None, None, "grp", "tile"),
            P(None, "grp", "tile"),
        ),
        check_vma=False,
    )
```

time: 58.5 us -> 47.8 us (0.82)
  the two profiles are of different devices: /device:TPU:54 before, /device:TPU:56 now
where the time goes in v2:
time: 47.8 us; the launch traced here: 47.6 us
  starting transfers between devices  33.4 us (70%)
  Pallas kernels  13.2 us (28%)
  between operations  0.78 us (2%)
    ppermute x3, starting transfers between devices, back(): return lax.ppermute(x, axis, [(i + 1, i) for i in range(count - 1)])  26.1 us
    ppermute x3, starting transfers between devices, ahead(): return lax.ppermute(x, axis, [(i, i + 1) for i in range(count - 1)])  7.34 us
    pallas_call x1, Pallas kernels, transport(): pl.pallas_call(main_kernel, out_shape=(f32(TRACERS, ROWS, LEVELS, LANES),...  5.78 us
    pallas_call x1, Pallas kernels, finish(): pl.pallas_call(finish_kernel, out_shape=(f32(4, LANES, LANES), bf16(TRACE...  5.56 us
    pallas_call x1, Pallas kernels, pack(): pl.pallas_call(pack_kernel, out_shape=(bf16(payload, LANES), bf16(payload...  1.89 us
  transfers between devices with their start and end apart: 6, of which 0 were waited for; matrix products, arithmetic and copies ran while one was open for 0% of the time, Pallas kernels for 12%

profile of v2, /device:TPU:56, one launch (start us, length us, event | category | flops | bytes accessed | tf_op | source)
XLA Modules:
  0.0 47.6 jit_solution(16292117637451790940)
XLA Ops:
  0.6 1.9 %pack.1 = (bf16[1920,128]{1,0:T(8,128)(2,1)S(1)}, bf16[1920,128]{1,0:T(8,128)(2,1)S(1)}, f32[4,128,128]{2,1,0:T(8,128)S(1)}, f32[128,128]{1,0:T(8,128)S(1)}) custom-call(bf16[10,128,128]{2,1,0:T(8,128)(2,1)} %bitcast.9, f32[4,128,128]{2,1,0:T(8,128)} %bitcast.10), custom_call_target="tpu_custom_call" | custom-call | tf_op jit(solution)/shard_map/pack/pallas_call | solution.py:498
  2.5 15.6 %collective-permute-start.2 = (f32[128,128]{1,0:T(8,128)S(1)}, f32[128,128]{1,0:T(8,128)S(1)}, u32[]{:S(2)}, u32[]{:S(2)}) collective-permute-start(f32[128,128]{1,0:T(8,128)S(1)} %get-tuple-element.21), channel_id=1, source_target_pairs={{1,0},{2,1},{3,2},{4,3},{5,4},{6,5},{7,6},{8,7},{9,8},{10,9},{11,1... | collective-permute-start | bytes 196616 | tf_op jit(solution)/shard_map/ppermute | solution.py:565
  18.1 1.9 %collective-permute-start.3 = (f32[128,128]{1,0:T(8,128)S(1)}, f32[128,128]{1,0:T(8,128)S(1)}, u32[]{:S(2)}, u32[]{:S(2)}) collective-permute-start(f32[128,128]{1,0:T(8,128)S(1)} %get-tuple-element.21), channel_id=1, source_target_pairs={{0,1},{1,2},{2,3},{3,4},{4,5},{5,6},{6,7},{7,8},{8,9},{9,10},{10,1... | collective-permute-start | bytes 196616 | tf_op jit(solution)/shard_map/ppermute | solution.py:562
  20.1 3.4 %collective-permute-start = (bf16[1920,128]{1,0:T(8,128)(2,1)S(1)}, bf16[1920,128]{1,0:T(8,128)(2,1)S(1)}, u32[]{:S(2)}, u32[]{:S(2)}) collective-permute-start(bf16[1920,128]{1,0:T(8,128)(2,1)S(1)} %get-tuple-element.14.mine), channel_id=1, source_target_pairs={{0,96},{96,192},{192,288},{288,384},{384,480},{480,576},{576,672},... | collective-permute-start | bytes 1474568 | tf_op jit(solution)/shard_map/ppermute | solution.py:562
  23.5 4.6 %collective-permute-start.1 = (bf16[1920,128]{1,0:T(8,128)(2,1)S(1)}, bf16[1920,128]{1,0:T(8,128)(2,1)S(1)}, u32[]{:S(2)}, u32[]{:S(2)}) collective-permute-start(bf16[1920,128]{1,0:T(8,128)(2,1)S(1)} %get-tuple-element.15), channel_id=1, source_target_pairs={{96,0},{192,96},{288,192},{384,288},{480,384},{576,480},{672,576},... | collective-permute-start | bytes 1474568 | tf_op jit(solution)/shard_map/ppermute | solution.py:565
  28.1 0.0 collective-permute-done.2
  28.1 0.0 collective-permute-done.3
  28.1 2.0 %collective-permute-start.4 = (f32[64,128]{1,0:T(8,128)S(1)}, f32[64,128]{1,0:T(8,128)S(1)}, u32[]{:S(2)}, u32[]{:S(2)}) collective-permute-start(f32[64,128]{1,0:T(8,128)S(1)} %get-tuple-element.26), channel_id=1, source_target_pairs={{0,96},{96,192},{192,288},{288,384},{384,480},{480,576},{576,672},... | collective-permute-start | bytes 98312 | tf_op jit(solution)/shard_map/ppermute | solution.py:562
  30.2 5.9 %collective-permute-start.5 = (f32[64,128]{1,0:T(8,128)S(1)}, f32[64,128]{1,0:T(8,128)S(1)}, u32[]{:S(2)}, u32[]{:S(2)}) collective-permute-start(f32[64,128]{1,0:T(8,128)S(1)} %get-tuple-element.25), channel_id=1, source_target_pairs={{96,0},{192,96},{288,192},{384,288},{480,384},{576,480},{672,576},... | collective-permute-start | bytes 98312 | tf_op jit(solution)/shard_map/ppermute | solution.py:565
  36.1 0.1 add_convert_fusion.flags
  36.2 0.0 collective-permute-done.before
  36.2 0.0 collective-permute-done.1.after
  36.2 5.8 %main.1 = (f32[10,4,32,128]{3,2,1,0:T(8,128)S(1)}, f32[4,4,32,128]{3,2,1,0:T(8,128)S(1)}, f32[2,3,128,128]{3,2,1,0:T(8,128)S(1)}, f32[36,32,128]{2,1,0:T(8,128)S(1)}) custom-call(f32[4]{0:T(128)S(1)} %add_convert_fusion.flags, bf16[1920,128]{1,0:T(8,128)(2,1)S(1)} %get-tuple-element.14.mine, bf16[1920,128]{1,0:T(8,128)(2,1)S(1)} %collective-permute-done.before, ...), custom_call_target="tpu_custom_call" | custom-call | flops 40000000 | bytes 4000000 | tf_op jit(solution)/shard_map/main/pallas_call | solution.py:514
  42.0 0.0 collective-permute-done.4.halo_before
  42.0 0.0 collective-permute-done.5.halo_after
  42.0 5.6 %finish.1 = (f32[4,128,128]{2,1,0:T(8,128)}, bf16[10,128,128]{2,1,0:T(8,128)(2,1)}, f32[128,128]{1,0:T(8,128)}) custom-call(f32[4]{0:T(128)S(1)} %add_convert_fusion.flags, f32[10,4,32,128]{3,2,1,0:T(8,128)S(1)} %get-tuple-element.17.two, f32[4,4,32,128]{3,2,1,0:T(8,128)S(1)} %get-tuple-element.18.ocean_two, f32[2,3,128,128]{3,2,1,0:T(8,128)S(1)} %get-tuple-element.19.strip, ...), custom_call_target="tpu_custom_call" | custom-call | tf_op jit(solution)/shard_map/finish/pallas_call | solution.py:532
  (4 shorter events, 0.0 us)
Async XLA Ops:
  2.5 25.6 %collective-permute-start.2 = (f32[128,128]{1,0:T(8,128)S(1)}, f32[128,128]{1,0:T(8,128)S(1)}, u32[]{:S(2)}, u32[]{:S(2)}) collective-permute-start(f32[128,128]{1,0:T(8,128)S(1)} %get-tuple-element.21), channel_id=1, source_target_pairs={{1,0},{2,1},{3,2},{4,3},{5,4},{6,5},{7,6},{8,7},{9,8},{10,9},{11,1... | collective-permute-start | bytes 196616 | tf_op jit(solution)/shard_map/ppermute | solution.py:565
  18.1 10.0 %collective-permute-start.3 = (f32[128,128]{1,0:T(8,128)S(1)}, f32[128,128]{1,0:T(8,128)S(1)}, u32[]{:S(2)}, u32[]{:S(2)}) collective-permute-start(f32[128,128]{1,0:T(8,128)S(1)} %get-tuple-element.21), channel_id=1, source_target_pairs={{0,1},{1,2},{2,3},{3,4},{4,5},{5,6},{6,7},{7,8},{8,9},{9,10},{10,1... | collective-permute-start | bytes 196616 | tf_op jit(solution)/shard_map/ppermute | solution.py:562
  20.1 16.1 %collective-permute-start = (bf16[1920,128]{1,0:T(8,128)(2,1)S(1)}, bf16[1920,128]{1,0:T(8,128)(2,1)S(1)}, u32[]{:S(2)}, u32[]{:S(2)}) collective-permute-start(bf16[1920,128]{1,0:T(8,128)(2,1)S(1)} %get-tuple-element.14.mine), channel_id=1, source_target_pairs={{0,96},{96,192},{192,288},{288,384},{384,480},{480,576},{576,672},... | collective-permute-start | bytes 1474568 | tf_op jit(solution)/shard_map/ppermute | solution.py:562
  23.5 12.7 %collective-permute-start.1 = (bf16[1920,128]{1,0:T(8,128)(2,1)S(1)}, bf16[1920,128]{1,0:T(8,128)(2,1)S(1)}, u32[]{:S(2)}, u32[]{:S(2)}) collective-permute-start(bf16[1920,128]{1,0:T(8,128)(2,1)S(1)} %get-tuple-element.15), channel_id=1, source_target_pairs={{96,0},{192,96},{288,192},{384,288},{480,384},{576,480},{672,576},... | collective-permute-start | bytes 1474568 | tf_op jit(solution)/shard_map/ppermute | solution.py:565
  28.1 13.8 %collective-permute-start.4 = (f32[64,128]{1,0:T(8,128)S(1)}, f32[64,128]{1,0:T(8,128)S(1)}, u32[]{:S(2)}, u32[]{:S(2)}) collective-permute-start(f32[64,128]{1,0:T(8,128)S(1)} %get-tuple-element.26), channel_id=1, source_target_pairs={{0,96},{96,192},{192,288},{288,384},{384,480},{480,576},{576,672},... | collective-permute-start | bytes 98312 | tf_op jit(solution)/shard_map/ppermute | solution.py:562
  30.2 11.8 %collective-permute-start.5 = (f32[64,128]{1,0:T(8,128)S(1)}, f32[64,128]{1,0:T(8,128)S(1)}, u32[]{:S(2)}, u32[]{:S(2)}) collective-permute-start(f32[64,128]{1,0:T(8,128)S(1)} %get-tuple-element.25), channel_id=1, source_target_pairs={{96,0},{192,96},{288,192},{384,288},{480,384},{576,480},{672,576},... | collective-permute-start | bytes 98312 | tf_op jit(solution)/shard_map/ppermute | solution.py:565

commit v3 on v2

--- a/solution.py
+++ b/solution.py
@@ -1,3 +1,7 @@
+import functools
+
+import functools
+
 import jax
 import jax.numpy as jnp
 from jax import lax
@@ -40,11 +44,20 @@
     FACES[_name] = (_count, _first)
     _count += _number
 FACE_SLOTS = _count
+SPEEDS = {
+    key: k
+    for k, key in enumerate(
+        [("u", "1", j) for j in range(-2, 6)]
+        + [("v", "1", j) for j in range(-3, 6)]
+        + [("u", "2", j) for j in range(4)]
+        + [("v", "2", j) for j in range(-1, 4)]
+    )
+}
 HALO_BEFORE = [(f, j) for f in (U, V) for j in (-3, -2, -1)] + [(f, j) for f in (T, S) for j in (-2, -1)]
 HALO_AFTER = [(f, j) for f in (U, V) for j in (4, 5, 6)] + [(f, j) for f in (T, S) for j in (4, 5)]
 HALO = {key: k for k, key in enumerate(HALO_BEFORE + HALO_AFTER)}
 STRIP = {key: k for k, key in enumerate([(f, j) for f in (U, V) for j in range(-3, 7)] + [(f, j) for f in (T, S) for j in range(-2, 6)])}
-PARTS = 2 * len(HALO_BEFORE)
+PARTS = 2 * 4 * ROWS
 
 
 def roll(x, shift, axis=1):
@@ -75,6 +88,12 @@
 
 def last_row(x):
     return jnp.broadcast_to(x[7:8, :], x.shape)
+
+
+def split_speed(faces, axis, stage, j, at, speed):
+    for sign, part in (("p", jnp.maximum), ("m", jnp.minimum)):
+        slot, first = FACES[axis + sign + stage]
+        faces[slot + j - first, at, :] = part(speed, 0.0)
 
 
 def tendency(q, big, j):
@@ -95,7 +114,7 @@
     return out
 
 
-def ocean_steps(load, faces, carry, store, up, down, lane_mask, spread):
+def ocean_steps(load, put_face, carry, store, up, down, lane_mask):
     sub = lax.broadcasted_iota(jnp.int32, (8, LANES), 0)
     carry[...] = jnp.zeros_like(carry)
     scale = 0.25 * time_step
@@ -104,10 +123,7 @@
         at = pl.ds(block * 8, 8)
 
         def speeds(stage, axis, j, a, b):
-            speed = spread(scale * (a + b))
-            for sign, part in (("p", jnp.maximum), ("m", jnp.minimum)):
-                slot, first = FACES[axis + sign + stage]
-                faces[slot + j - first, at, :] = part(speed, 0.0)
+            put_face(axis, stage, j, at, scale * (a + b))
 
         def depth_sum(q, rows, base):
             big = {}
@@ -217,7 +233,12 @@
     return slice(y * LEVELS, (y + 1) * LEVELS)
 
 
-def pack_kernel(tr, oc, to_next, to_previous, own_ocean, edges, tracer_in, ocean_in, sems):
+def part_rows(f, y, part):
+    first = TRACERS * LANES + ((f * ROWS + y) * 2 + part) * LEVELS
+    return slice(first, first + LEVELS)
+
+
+def pack_kernel(tr, oc, mine, own_ocean, edges, tracer_in, ocean_in, sems):
     half = pl.ds(0, COPIES), pl.ds(COPIES, COPIES)
     copies = [pltpu.make_async_copy(tr.at[half[k]], tracer_in.at[half[k]], sems.at[k]) for k in range(2)]
     copies.append(pltpu.make_async_copy(oc, ocean_in, sems.at[2]))
@@ -225,7 +246,8 @@
         copy.start()
     row, lane = whole_iota(0), whole_iota(1)
     reorder = one_hot(lane == (row % LEVELS) * ROWS + row // LEVELS)
-    acc = jnp.zeros((LANES, LANES), jnp.float32)
+    source = jnp.where(row < 4, row + 8, jnp.where(row >= LANES - 4, row - (LANES - 16), -4 * LANES))
+    edge = None
 
     def with_edges(acc, x, base):
         acc = jnp.where((lane >= base) & (lane < base + 4), roll(x, base), acc)
@@ -235,41 +257,35 @@
         if k % COPIES == 0:
             copies[k // COPIES].wait()
         x = jnp.dot(reorder, tracer_in[k], preferred_element_type=jnp.float32)
-        narrow = x.astype(jnp.bfloat16)
-        to_next[k * LANES : (k + 1) * LANES, :] = narrow
-        to_previous[k * LANES : (k + 1) * LANES, :] = narrow
-        acc = with_edges(acc, x, GROUP * (k % COPIES) + 8 + 8 * (k // COPIES))
-    base = TRACERS * LANES
+        mine[k * LANES : (k + 1) * LANES, :] = x.astype(jnp.bfloat16)
+        here = GROUP * (k % COPIES) + 8 * (k // COPIES)
+        term = jnp.dot(tracer_in[k], one_hot(lane == source + here), preferred_element_type=jnp.float32)
+        edge = term if edge is None else edge + term
+    acc = jnp.dot(reorder, edge.astype(jnp.bfloat16), preferred_element_type=jnp.float32)
     copies[2].wait()
     for f in range(4):
-        levels = []
         for y in range(ROWS):
             x = ocean_in[f, pl.ds(y, LEVELS, stride=ROWS), :]
             own_ocean[f, level_rows(y), :] = x
             high = x.astype(jnp.bfloat16)
-            low = (x - high.astype(jnp.float32)).astype(jnp.bfloat16)
-            levels.append((high, low))
+            mine[part_rows(f, y, 0), :] = high
+            mine[part_rows(f, y, 1), :] = (x - high.astype(jnp.float32)).astype(jnp.bfloat16)
         acc = with_edges(acc, own_ocean[f], GROUP * f)
-        wanted = ((1, 2, 3), (0, 1, 2)) if f in (U, V) else ((2, 3), (0, 1))
-        parts = [[part for y in rows for part in levels[y]] for rows in wanted]
-        for out, side in zip((to_next, to_previous), parts):
-            for k, part in enumerate(side):
-                out[base + k * LEVELS : base + (k + 1) * LEVELS, :] = part
-        base += len(parts[0]) * LEVELS
     edges[...] = acc
 
 
-def main_kernel(flags, mine, before, after, own_ocean, two, ocean_two, strip, ocean_strip, faces, carry, halo):
-    up, down = flags[0], flags[1]
-    sides = (before, mine, after)
-    for side, names in ((before, HALO_BEFORE), (after, HALO_AFTER)):
-
-        def part(k):
-            at = TRACERS * LANES + k * LEVELS
-            return side[at : at + LEVELS, :].astype(jnp.float32)
-
-        for k, key in enumerate(names):
-            halo[HALO[key]] = part(2 * k) + part(2 * k + 1)
+def main_kernel(flags, mine, near, far, own_ocean, two, ocean_two, strip, ocean_strip, faces, carry, halo):
+    up, down, even = flags[0], flags[1], flags[4] > 0.5
+
+    def side(tile, at):
+        if tile == 1:
+            return mine[at, :]
+        first, second = (far, near) if tile == 0 else (near, far)
+        return jnp.where(even, first[at, :], second[at, :])
+
+    for (f, j), k in HALO.items():
+        parts = [side((j + ROWS) // ROWS, part_rows(f, j % ROWS, part)).astype(jnp.float32) for part in range(2)]
+        halo[k] = parts[0] + parts[1]
 
     def load(f, j, at):
         if 0 <= j < ROWS:
@@ -279,7 +295,7 @@
     def store(f, j, at, value):
         ocean_two[f, j, at, :] = value
 
-    ocean_steps(load, faces, carry, store, up, down, None, lambda x: x)
+    ocean_steps(load, functools.partial(split_speed, faces), carry, store, up, down, None)
 
     def body(t, _):
         for part in range(LEVELS // 16):
@@ -288,7 +304,7 @@
                 def cell(j):
                     y = (j + 4) % 4
                     at = pl.multiple_of(t * LANES + y * LEVELS + part * 16, 16)
-                    return sides[(j + 4) // 4][pl.ds(at, 16), :].astype(jnp.float32)[half * 8 : half * 8 + 8]
+                    return side((j + 4) // 4, pl.ds(at, 16)).astype(jnp.float32)[half * 8 : half * 8 + 8]
 
                 at = slice(part * 16 + half * 8, part * 16 + half * 8 + 8)
 
@@ -308,7 +324,7 @@
             acc = None
             for k in range(COPIES):
                 at = (half * COPIES + k) * LANES
-                term = jnp.dot(sides[tile][at : at + LANES, :], picks[k], preferred_element_type=jnp.float32)
+                term = jnp.dot(side(tile, slice(at, at + LANES)), picks[k], preferred_element_type=jnp.float32)
                 acc = term if acc is None else acc + term
             strip[half, tile] = acc
     lanes = lax.broadcasted_iota(jnp.int32, (LEVELS, LANES), 1)
@@ -319,8 +335,8 @@
 
 
 def finish_kernel(
-    flags, two, ocean_two, strip, ocean_strip, halo, halo_before, halo_after, rates_in, wet_in, light_in,
-    ocean_out, tracer_out, heating, faces, carry, cells, strip_two, strip_ocean, reacted, narrow, ocean_done, heat_done,
+    flags, two, ocean_two, strip, ocean_strip, from_left, from_right, rates_in, wet_in, light_in,
+    ocean_out, tracer_out, heating, faces, carry, raw, halo, cells, strip_two, strip_ocean, reacted, narrow, ocean_done, heat_done,
     rates, wet_blocks, light, sems,
 ):
     small = [
@@ -332,12 +348,8 @@
     up, down, left, right = (flags[k] for k in range(4))
     lanes = lax.broadcasted_iota(jnp.int32, (LEVELS, LANES), 1)
 
-    def halo_row(j):
-        if j < 0:
-            return halo_before[level_rows(j + 2), :]
-        if j < ROWS:
-            return halo[level_rows(j), :]
-        return halo_after[level_rows(j - ROWS), :]
+    from_one = lax.broadcasted_iota(jnp.int32, halo.shape, 1) % 8 < 4
+    halo[...] = jnp.where(from_one, from_right[...], from_left[...])
 
     middle = (lanes % GROUP >= 8) & (lanes % GROUP < 16)
     for j in range(-4, 8):
@@ -345,12 +357,11 @@
         for half in range(2):
             x = strip[half, tile, level_rows(y), :]
             if -2 <= j < 6:
-                fresh = halo_row(j)
+                fresh = halo[level_rows(j + 2), :]
                 x = jnp.where(middle, roll(fresh, -8) if half else fresh, x)
             cells[half, j + 4] = x
 
     place_in = lax.broadcasted_iota(jnp.int32, (8, LANES), 1)
-    first_group = place_in < GROUP
     first_middle = (place_in >= 8) & (place_in < 16)
     place_in = place_in % GROUP
     lane_mask = jnp.where((place_in >= 8) & (place_in < 12), right, jnp.where((place_in >= 12) & (place_in < 16), left, 1.0))
@@ -358,24 +369,26 @@
     def load(f, j, at):
         x = ocean_strip[STRIP[f, j], at, :]
         if -2 <= j < 6:
-            if j < 0:
-                fresh = halo_before[pl.ds(at.start + (j + 2) * LEVELS, 8), :]
-            elif j < ROWS:
-                fresh = halo[pl.ds(at.start + j * LEVELS, 8), :]
-            else:
-                fresh = halo_after[pl.ds(at.start + (j - ROWS) * LEVELS, 8), :]
+            fresh = halo[pl.ds(at.start + (j + 2) * LEVELS, 8), :]
             x = jnp.where(first_middle, roll(fresh, 8 - GROUP * f), x)
         return x
 
     def store(f, j, at, value):
         strip_ocean[f, j, at, :] = value
 
-    def spread(x):
-        x = jnp.where(first_group, x, 0.0)
-        pair = x + roll(x, GROUP)
-        return pair + roll(pair, 2 * GROUP) + roll(x, 4 * GROUP)
-
-    ocean_steps(load, faces, carry, store, up, down, lane_mask, spread)
+    def keep(axis, stage, j, at, speed):
+        raw[SPEEDS[axis, stage, j], at, :] = speed
+
+    ocean_steps(load, keep, carry, store, up, down, lane_mask)
+    row, whole_lane = whole_iota(0), whole_iota(1)
+    copy_out = one_hot((row < GROUP) & (whole_lane % GROUP == row) & (whole_lane < GROUP * COPIES))
+    copy_out = jnp.concatenate([copy_out, copy_out], axis=0)
+    for axis, stage, j in SPEEDS:
+        x = raw[SPEEDS[axis, stage, j]]
+        high = x.astype(jnp.bfloat16)
+        low = (x - high.astype(jnp.float32)).astype(jnp.bfloat16)
+        speed = jnp.dot(jnp.concatenate([high, low], axis=1), copy_out, preferred_element_type=jnp.float32)
+        split_speed(faces, axis, stage, j, slice(0, LEVELS), speed)
 
     def body(block, _):
         at = pl.ds(block * 8, 8)
@@ -387,7 +400,7 @@
             tracer_steps(lambda j: cells[half, j + 4, at, :], faces, at, up, down, lane_mask, put)
         return 0
 
-    lax.fori_loop(0, BLOCKS, body, 0)
+    lax.fori_loop(0, BLOCKS, body, 0, unroll=2)
     for copy in small:
         copy.wait()
     lane = lax.broadcasted_iota(jnp.int32, (8, LANES), 1)
@@ -497,9 +510,9 @@
     payload = TRACERS * LANES + PARTS * LEVELS
     return pl.pallas_call(
         pack_kernel,
-        out_shape=(bf16(payload, LANES), bf16(payload, LANES), f32(4, LANES, LANES), f32(LANES, LANES)),
+        out_shape=(bf16(payload, LANES), f32(4, LANES, LANES), f32(LANES, LANES)),
         in_specs=hbm(2),
-        out_specs=vmem(4),
+        out_specs=vmem(3),
         scratch_shapes=[
             pltpu.VMEM((TRACERS, LANES, LANES), jnp.bfloat16),
             pltpu.VMEM((4, LANES, LANES), jnp.float32),
@@ -510,7 +523,7 @@
     )(in_hbm(tr), in_hbm(oc))
 
 
-def transport(flags, mine, before, after, own_ocean):
+def transport(flags, mine, near, far, own_ocean):
     return pl.pallas_call(
         main_kernel,
         out_shape=(
@@ -525,17 +538,19 @@
         cost_estimate=cost(40_000_000, 4_000_000),
         compiler_params=limit(8),
         name="main",
-    )(flags, mine, before, after, own_ocean)
+    )(flags, mine, near, far, own_ocean)
 
 
 def finish(flags, main, halos, rates, wet_blocks, surface_light):
     return pl.pallas_call(
         finish_kernel,
         out_shape=(f32(4, LANES, LANES), bf16(TRACERS, LANES, LANES), f32(LANES, LANES)),
-        in_specs=smem(1) + vmem(7) + hbm(3),
+        in_specs=smem(1) + vmem(6) + hbm(3),
         out_specs=hbm(3),
         scratch_shapes=STEP_SCRATCH
         + [
+            pltpu.VMEM((len(SPEEDS), LEVELS, LANES), jnp.float32),
+            pltpu.VMEM((2 * LANES, LANES), jnp.float32),
             pltpu.VMEM((2, 12, LEVELS, LANES), jnp.float32),
             pltpu.VMEM((2, ROWS, LEVELS, LANES), jnp.float32),
             pltpu.VMEM((4, ROWS, LEVELS, LANES), jnp.float32),
@@ -564,20 +579,24 @@
     def back(x, axis, count):
         return lax.ppermute(x, axis, [(i + 1, i) for i in range(count - 1)])
 
+    within = [(i, i ^ 1) for i in range(groups) if i ^ 1 < groups]
+    between = [pair for i in range(1, groups - 1, 2) for pair in ((i, i + 1), (i + 1, i))]
     g, t = lax.axis_index("grp"), lax.axis_index("tile")
-    flags = jnp.stack([g > 0, g < groups - 1, t > 0, t < tiles - 1]).astype(jnp.float32)
-    to_next, to_previous, own_ocean, edges = pack(tr, oc)
+    flags = jnp.stack([g > 0, g < groups - 1, t > 0, t < tiles - 1, g % 2 == 0]).astype(jnp.float32)
+    mine, own_ocean, edges = pack(tr, oc)
+    edges_far = lax.ppermute(edges, "grp", between)
+    edges_near = lax.ppermute(edges, "grp", within)
+    far = lax.ppermute(mine, "grp", between)
+    near = lax.ppermute(mine, "grp", within)
+    even, half = g % 2 == 0, 2 * LEVELS
+    edges_before = jnp.where(even, edges_far[half:], edges_near[half:])
+    edges_after = jnp.where(even, edges_near[:half], edges_far[:half])
+    edges = jnp.concatenate([edges_before, edges, edges_after], axis=0)
     from_left = ahead(edges, "tile", tiles)
-    before = ahead(to_next, "grp", groups)
-    after = back(to_previous, "grp", groups)
     from_right = back(edges, "tile", tiles)
-    lane = lax.broadcasted_iota(jnp.int32, (LANES, LANES), 1)
-    halo = jnp.where(lane % 8 < 4, from_right, from_left)
-    halo_before = ahead(halo[2 * LEVELS :], "grp", groups)
-    halo_after = back(halo[: 2 * LEVELS], "grp", groups)
-    main = transport(flags, to_next, before, after, own_ocean)
+    main = transport(flags, mine, near, far, own_ocean)
     ocean_out, tracer_out, heating = finish(
-        flags, main, (halo, halo_before, halo_after), rates, wet_blocks, surface_light
+        flags, main, (from_left, from_right), rates, wet_blocks, surface_light
     )
     return (
         ocean_out.reshape(ocean.shape),

time: 47.8 us -> 53.6 us (1.12)
  waiting for transfers between devices: 0.02 us -> 10.3 us
  starting transfers between devices: 33.4 us -> 29.6 us
  Pallas kernels: 13.2 us -> 12.5 us
    ppermute x0 -> x4, starting transfers between devices: none -> 13.3 us  [the longest x1 4.8 us: shards(): far = lax.ppermute(mine, 'grp', between)]
    ppermute x3 -> x1, starting transfers between devices: 26.1 us -> 14.5 us  [back(): return lax.ppermute(x, axis, [(i + 1, i) for i in range(count - 1)])]
    ppermute x0 -> x4, waiting for transfers between devices: none -> 10.3 us  [the longest x1 5.24 us: shards(): edges_far = lax.ppermute(edges, 'grp', between)]
    ppermute x3 -> x1, starting transfers between devices: 7.34 us -> 1.92 us  [ahead(): return lax.ppermute(x, axis, [(i, i + 1) for i in range(count - 1)])]
  transfers between devices with their start and end apart: 6 -> 6, of which waited for: 0 -> 2; matrix products, arithmetic and copies ran while one was open for 0% -> 0% of each run, Pallas kernels for 12% -> 11%
where the time goes in v3:
time: 53.6 us; the launch traced here: 53.4 us
  starting transfers between devices  29.6 us (55%)
  Pallas kernels  12.5 us (23%)
  waiting for transfers between devices  10.3 us (19%)
  between operations  0.76 us (1%)
    ppermute x1, starting transfers between devices, back(): return lax.ppermute(x, axis, [(i + 1, i) for i in range(count - 1)])  14.5 us
    pallas_call x1, Pallas kernels, transport(): pl.pallas_call(main_kernel, out_shape=(f32(TRACERS, ROWS, LEVELS, LANES),...  5.69 us
    ppermute x1, waiting for transfers between devices, shards(): edges_far = lax.ppermute(edges, 'grp', between)  5.24 us
    pallas_call x1, Pallas kernels, finish(): pl.pallas_call(finish_kernel, out_shape=(f32(4, LANES, LANES), bf16(TRACE...  5.11 us
    ppermute x1, waiting for transfers between devices, shards(): edges_near = lax.ppermute(edges, 'grp', within)  5.05 us
    ppermute x1, starting transfers between devices, shards(): far = lax.ppermute(mine, 'grp', between)  4.8 us
    ppermute x1, starting transfers between devices, shards(): near = lax.ppermute(mine, 'grp', within)  3.39 us
    ppermute x1, starting transfers between devices, shards(): edges_far = lax.ppermute(edges, 'grp', between)  3.16 us
  transfers between devices with their start and end apart: 6, of which 2 were waited for; matrix products, arithmetic and copies ran while one was open for 0% of the time, Pallas kernels for 11%

profile of v3, /device:TPU:56, one launch (start us, length us, event | category | flops | bytes accessed | tf_op | source)
XLA Modules:
  0.0 53.4 jit_solution(12026921834105713184)
XLA Ops:
  0.6 1.7 %pack.1 = (bf16[2304,128]{1,0:T(8,128)(2,1)S(1)}, f32[4,128,128]{2,1,0:T(8,128)S(1)}, f32[128,128]{1,0:T(8,128)S(1)}) custom-call(bf16[10,128,128]{2,1,0:T(8,128)(2,1)} %bitcast.10, f32[4,128,128]{2,1,0:T(8,128)} %bitcast.11), custom_call_target="tpu_custom_call" | custom-call | tf_op jit(solution)/shard_map/pack/pallas_call | solution.py:511
  2.4 3.4 %collective-permute-start = (bf16[2304,128]{1,0:T(8,128)(2,1)S(1)}, bf16[2304,128]{1,0:T(8,128)(2,1)S(1)}, u32[]{:S(2)}, u32[]{:S(2)}) collective-permute-start(bf16[2304,128]{1,0:T(8,128)(2,1)S(1)} %get-tuple-element.13.mine), channel_id=1, source_target_pairs={{0,96},{96,0},{192,288},{288,192},{384,480},{480,384},{576,672},{6... | collective-permute-start | bytes 1769480 | tf_op jit(solution)/shard_map/ppermute | solution.py:590
  5.8 4.8 %collective-permute-start.1 = (bf16[2304,128]{1,0:T(8,128)(2,1)S(1)}, bf16[2304,128]{1,0:T(8,128)(2,1)S(1)}, u32[]{:S(2)}, u32[]{:S(2)}) collective-permute-start(bf16[2304,128]{1,0:T(8,128)(2,1)S(1)} %get-tuple-element.13.mine), channel_id=1, source_target_pairs={{96,192},{192,96},{288,384},{384,288},{480,576},{576,480},{97,193}... | collective-permute-start | bytes 1769480 | tf_op jit(solution)/shard_map/ppermute | solution.py:589
  10.6 1.9 %collective-permute-start.3 = (f32[128,128]{1,0:T(8,128)S(1)}, f32[128,128]{1,0:T(8,128)S(1)}, u32[]{:S(2)}, u32[]{:S(2)}) collective-permute-start(f32[128,128]{1,0:T(8,128)S(1)} %get-tuple-element.19), channel_id=1, source_target_pairs={{0,96},{96,0},{192,288},{288,192},{384,480},{480,384},{576,672},{6... | collective-permute-start | bytes 196616 | tf_op jit(solution)/shard_map/ppermute | solution.py:588
  12.5 3.2 %collective-permute-start.2 = (f32[128,128]{1,0:T(8,128)S(1)}, f32[128,128]{1,0:T(8,128)S(1)}, u32[]{:S(2)}, u32[]{:S(2)}) collective-permute-start(f32[128,128]{1,0:T(8,128)S(1)} %get-tuple-element.19), channel_id=1, source_target_pairs={{96,192},{192,96},{288,384},{384,288},{480,576},{576,480},{97,193}... | collective-permute-start | bytes 196616 | tf_op jit(solution)/shard_map/ppermute | solution.py:587
  15.7 5.1 %collective-permute-done.3 = f32[128,128]{1,0:T(8,128)S(1)} collective-permute-done((f32[128,128]{1,0:T(8,128)S(1)}, f32[128,128]{1,0:T(8,128)S(1)}, u32[]{:S(2)}, u32[]{:S(2)}) %collective-permute-start.3) | collective-permute-done | bytes 65568 | tf_op jit(solution)/shard_map/ppermute | solution.py:588
  20.7 5.2 %collective-permute-done.2 = f32[128,128]{1,0:T(8,128)S(1)} collective-permute-done((f32[128,128]{1,0:T(8,128)S(1)}, f32[128,128]{1,0:T(8,128)S(1)}, u32[]{:S(2)}, u32[]{:S(2)}) %collective-permute-start.2) | collective-permute-done | bytes 65568 | tf_op jit(solution)/shard_map/ppermute | solution.py:587
  26.0 1.9 %collective-permute-start.4 = (f32[256,128]{1,0:T(8,128)S(1)}, f32[256,128]{1,0:T(8,128)S(1)}, u32[]{:S(2)}, u32[]{:S(2)}) collective-permute-start(f32[256,128]{1,0:T(8,128)S(1)} %pad_maximum_fusion), channel_id=1, source_target_pairs={{0,1},{1,2},{2,3},{3,4},{4,5},{5,6},{6,7},{7,8},{8,9},{9,10},{10,1... | collective-permute-start | bytes 393224 | tf_op jit(solution)/shard_map/ppermute | solution.py:577
  27.9 14.5 %collective-permute-start.5 = (f32[256,128]{1,0:T(8,128)S(1)}, f32[256,128]{1,0:T(8,128)S(1)}, u32[]{:S(2)}, u32[]{:S(2)}) collective-permute-start(f32[256,128]{1,0:T(8,128)S(1)} %pad_maximum_fusion), channel_id=1, source_target_pairs={{1,0},{2,1},{3,2},{4,3},{5,4},{6,5},{7,6},{8,7},{9,8},{10,9},{11,1... | collective-permute-start | bytes 393224 | tf_op jit(solution)/shard_map/ppermute | solution.py:580
  42.4 0.1 stack.23
  42.5 0.0 collective-permute-done.near
  42.5 0.0 collective-permute-done.1.far
  42.5 5.7 %main.1 = (f32[10,4,32,128]{3,2,1,0:T(8,128)S(1)}, f32[4,4,32,128]{3,2,1,0:T(8,128)S(1)}, f32[2,3,128,128]{3,2,1,0:T(8,128)S(1)}, f32[36,32,128]{2,1,0:T(8,128)S(1)}) custom-call(f32[5]{0:T(128)S(1)} %convert_element_type.3.flags, bf16[2304,128]{1,0:T(8,128)(2,1)S(1)} %get-tuple-element.13.mine, bf16[2304,128]{1,0:T(8,128)(2,1)S(1)} %collective-permute-done.near, ...), custom_call_target="tpu_custom_call" | custom-call | flops 40000000 | bytes 4000000 | tf_op jit(solution)/shard_map/main/pallas_call | solution.py:527
  48.2 0.0 collective-permute-done.4.from_left
  48.2 0.0 collective-permute-done.5.from_right
  48.3 5.1 %finish.1 = (f32[4,128,128]{2,1,0:T(8,128)}, bf16[10,128,128]{2,1,0:T(8,128)(2,1)}, f32[128,128]{1,0:T(8,128)}) custom-call(f32[5]{0:T(128)S(1)} %convert_element_type.3.flags, f32[10,4,32,128]{3,2,1,0:T(8,128)S(1)} %get-tuple-element.15.two, f32[4,4,32,128]{3,2,1,0:T(8,128)S(1)} %get-tuple-element.16.ocean_two, ...), custom_call_target="tpu_custom_call" | custom-call | tf_op jit(solution)/shard_map/finish/pallas_call | solution.py:545
  (3 shorter events, 0.0 us)
Async XLA Ops:
  2.4 40.2 %collective-permute-start = (bf16[2304,128]{1,0:T(8,128)(2,1)S(1)}, bf16[2304,128]{1,0:T(8,128)(2,1)S(1)}, u32[]{:S(2)}, u32[]{:S(2)}) collective-permute-start(bf16[2304,128]{1,0:T(8,128)(2,1)S(1)} %get-tuple-element.13.mine), channel_id=1, source_target_pairs={{0,96},{96,0},{192,288},{288,192},{384,480},{480,384},{576,672},{6... | collective-permute-start | bytes 1769480 | tf_op jit(solution)/shard_map/ppermute | solution.py:590
  5.8 36.8 %collective-permute-start.1 = (bf16[2304,128]{1,0:T(8,128)(2,1)S(1)}, bf16[2304,128]{1,0:T(8,128)(2,1)S(1)}, u32[]{:S(2)}, u32[]{:S(2)}) collective-permute-start(bf16[2304,128]{1,0:T(8,128)(2,1)S(1)} %get-tuple-element.13.mine), channel_id=1, source_target_pairs={{96,192},{192,96},{288,384},{384,288},{480,576},{576,480},{97,193}... | collective-permute-start | bytes 1769480 | tf_op jit(solution)/shard_map/ppermute | solution.py:589
  10.6 10.2 %collective-permute-start.3 = (f32[128,128]{1,0:T(8,128)S(1)}, f32[128,128]{1,0:T(8,128)S(1)}, u32[]{:S(2)}, u32[]{:S(2)}) collective-permute-start(f32[128,128]{1,0:T(8,128)S(1)} %get-tuple-element.19), channel_id=1, source_target_pairs={{0,96},{96,0},{192,288},{288,192},{384,480},{480,384},{576,672},{6... | collective-permute-start | bytes 196616 | tf_op jit(solution)/shard_map/ppermute | solution.py:588
  12.5 13.5 %collective-permute-start.2 = (f32[128,128]{1,0:T(8,128)S(1)}, f32[128,128]{1,0:T(8,128)S(1)}, u32[]{:S(2)}, u32[]{:S(2)}) collective-permute-start(f32[128,128]{1,0:T(8,128)S(1)} %get-tuple-element.19), channel_id=1, source_target_pairs={{96,192},{192,96},{288,384},{384,288},{480,576},{576,480},{97,193}... | collective-permute-start | bytes 196616 | tf_op jit(solution)/shard_map/ppermute | solution.py:587
  26.0 22.2 %collective-permute-start.4 = (f32[256,128]{1,0:T(8,128)S(1)}, f32[256,128]{1,0:T(8,128)S(1)}, u32[]{:S(2)}, u32[]{:S(2)}) collective-permute-start(f32[256,128]{1,0:T(8,128)S(1)} %pad_maximum_fusion), channel_id=1, source_target_pairs={{0,1},{1,2},{2,3},{3,4},{4,5},{5,6},{6,7},{7,8},{8,9},{9,10},{10,1... | collective-permute-start | bytes 393224 | tf_op jit(solution)/shard_map/ppermute | solution.py:577
  27.9 20.3 %collective-permute-start.5 = (f32[256,128]{1,0:T(8,128)S(1)}, f32[256,128]{1,0:T(8,128)S(1)}, u32[]{:S(2)}, u32[]{:S(2)}) collective-permute-start(f32[256,128]{1,0:T(8,128)S(1)} %pad_maximum_fusion), channel_id=1, source_target_pairs={{1,0},{2,1},{3,2},{4,3},{5,4},{6,5},{7,6},{8,7},{9,8},{10,9},{11,1... | collective-permute-start | bytes 393224 | tf_op jit(solution)/shard_map/ppermute | solution.py:580

commit v4 on v3

--- a/solution.py
+++ b/solution.py
@@ -164,7 +164,7 @@
                 store(f, j, at, 0.5 * (q[f][j] + one[f][j] + time_step * rate[f]))
         return 0
 
-    lax.fori_loop(0, BLOCKS, body, 0)
+    lax.fori_loop(0, BLOCKS, body, 0, unroll=2)
 
 
 def advance(c, low, high, face, finish):
@@ -383,12 +383,14 @@
     row, whole_lane = whole_iota(0), whole_iota(1)
     copy_out = one_hot((row < GROUP) & (whole_lane % GROUP == row) & (whole_lane < GROUP * COPIES))
     copy_out = jnp.concatenate([copy_out, copy_out], axis=0)
-    for axis, stage, j in SPEEDS:
-        x = raw[SPEEDS[axis, stage, j]]
+    names = list(SPEEDS)
+    for first in range(0, len(names), 13):
+        x = jnp.concatenate([raw[k] for k in range(first, first + 13)], axis=0)
         high = x.astype(jnp.bfloat16)
         low = (x - high.astype(jnp.float32)).astype(jnp.bfloat16)
         speed = jnp.dot(jnp.concatenate([high, low], axis=1), copy_out, preferred_element_type=jnp.float32)
-        split_speed(faces, axis, stage, j, slice(0, LEVELS), speed)
+        for k in range(13):
+            split_speed(faces, *names[first + k], slice(0, LEVELS), speed[k * LEVELS : (k + 1) * LEVELS])
 
     def body(block, _):
         at = pl.ds(block * 8, 8)

time: 53.6 us -> 53.2 us (level)
  no operation moved by 1% of the time
where the time goes in v4:
time: 53.2 us; the launch traced here: 53 us
  starting transfers between devices  29.6 us (56%)
  Pallas kernels  12.1 us (23%)
  waiting for transfers between devices  10.3 us (19%)
  between operations  0.76 us (1%)
    ppermute x1, starting transfers between devices, back(): return lax.ppermute(x, axis, [(i + 1, i) for i in range(count - 1)])  14.5 us
    pallas_call x1, Pallas kernels, transport(): pl.pallas_call(main_kernel, out_shape=(f32(TRACERS, ROWS, LEVELS, LANES),...  5.58 us
    ppermute x1, waiting for transfers between devices, shards(): edges_far = lax.ppermute(edges, 'grp', between)  5.24 us
    ppermute x1, waiting for transfers between devices, shards(): edges_near = lax.ppermute(edges, 'grp', within)  5.05 us
    pallas_call x1, Pallas kernels, finish(): pl.pallas_call(finish_kernel, out_shape=(f32(4, LANES, LANES), bf16(TRACE...  4.82 us
    ppermute x1, starting transfers between devices, shards(): far = lax.ppermute(mine, 'grp', between)  4.8 us
    ppermute x1, starting transfers between devices, shards(): near = lax.ppermute(mine, 'grp', within)  3.39 us
    ppermute x1, starting transfers between devices, shards(): edges_far = lax.ppermute(edges, 'grp', between)  3.16 us
  transfers between devices with their start and end apart: 6, of which 2 were waited for; matrix products, arithmetic and copies ran while one was open for 0% of the time, Pallas kernels for 11%

profile of v4, /device:TPU:56, one launch (start us, length us, event | category | flops | bytes accessed | tf_op | source)
XLA Modules:
  0.0 53.0 jit_solution(8373112780526545625)
XLA Ops:
  0.6 1.7 %pack.1 = (bf16[2304,128]{1,0:T(8,128)(2,1)S(1)}, f32[4,128,128]{2,1,0:T(8,128)S(1)}, f32[128,128]{1,0:T(8,128)S(1)}) custom-call(bf16[10,128,128]{2,1,0:T(8,128)(2,1)} %bitcast.10, f32[4,128,128]{2,1,0:T(8,128)} %bitcast.11), custom_call_target="tpu_custom_call" | custom-call | tf_op jit(solution)/shard_map/pack/pallas_call | solution.py:513
  2.4 3.4 %collective-permute-start = (bf16[2304,128]{1,0:T(8,128)(2,1)S(1)}, bf16[2304,128]{1,0:T(8,128)(2,1)S(1)}, u32[]{:S(2)}, u32[]{:S(2)}) collective-permute-start(bf16[2304,128]{1,0:T(8,128)(2,1)S(1)} %get-tuple-element.13.mine), channel_id=1, source_target_pairs={{0,96},{96,0},{192,288},{288,192},{384,480},{480,384},{576,672},{6... | collective-permute-start | bytes 1769480 | tf_op jit(solution)/shard_map/ppermute | solution.py:592
  5.8 4.8 %collective-permute-start.1 = (bf16[2304,128]{1,0:T(8,128)(2,1)S(1)}, bf16[2304,128]{1,0:T(8,128)(2,1)S(1)}, u32[]{:S(2)}, u32[]{:S(2)}) collective-permute-start(bf16[2304,128]{1,0:T(8,128)(2,1)S(1)} %get-tuple-element.13.mine), channel_id=1, source_target_pairs={{96,192},{192,96},{288,384},{384,288},{480,576},{576,480},{97,193}... | collective-permute-start | bytes 1769480 | tf_op jit(solution)/shard_map/ppermute | solution.py:591
  10.6 1.9 %collective-permute-start.3 = (f32[128,128]{1,0:T(8,128)S(1)}, f32[128,128]{1,0:T(8,128)S(1)}, u32[]{:S(2)}, u32[]{:S(2)}) collective-permute-start(f32[128,128]{1,0:T(8,128)S(1)} %get-tuple-element.19), channel_id=1, source_target_pairs={{0,96},{96,0},{192,288},{288,192},{384,480},{480,384},{576,672},{6... | collective-permute-start | bytes 196616 | tf_op jit(solution)/shard_map/ppermute | solution.py:590
  12.5 3.2 %collective-permute-start.2 = (f32[128,128]{1,0:T(8,128)S(1)}, f32[128,128]{1,0:T(8,128)S(1)}, u32[]{:S(2)}, u32[]{:S(2)}) collective-permute-start(f32[128,128]{1,0:T(8,128)S(1)} %get-tuple-element.19), channel_id=1, source_target_pairs={{96,192},{192,96},{288,384},{384,288},{480,576},{576,480},{97,193}... | collective-permute-start | bytes 196616 | tf_op jit(solution)/shard_map/ppermute | solution.py:589
  15.7 5.1 %collective-permute-done.3 = f32[128,128]{1,0:T(8,128)S(1)} collective-permute-done((f32[128,128]{1,0:T(8,128)S(1)}, f32[128,128]{1,0:T(8,128)S(1)}, u32[]{:S(2)}, u32[]{:S(2)}) %collective-permute-start.3) | collective-permute-done | bytes 65568 | tf_op jit(solution)/shard_map/ppermute | solution.py:590
  20.7 5.2 %collective-permute-done.2 = f32[128,128]{1,0:T(8,128)S(1)} collective-permute-done((f32[128,128]{1,0:T(8,128)S(1)}, f32[128,128]{1,0:T(8,128)S(1)}, u32[]{:S(2)}, u32[]{:S(2)}) %collective-permute-start.2) | collective-permute-done | bytes 65568 | tf_op jit(solution)/shard_map/ppermute | solution.py:589
  26.0 1.9 %collective-permute-start.4 = (f32[256,128]{1,0:T(8,128)S(1)}, f32[256,128]{1,0:T(8,128)S(1)}, u32[]{:S(2)}, u32[]{:S(2)}) collective-permute-start(f32[256,128]{1,0:T(8,128)S(1)} %pad_maximum_fusion), channel_id=1, source_target_pairs={{0,1},{1,2},{2,3},{3,4},{4,5},{5,6},{6,7},{7,8},{8,9},{9,10},{10,1... | collective-permute-start | bytes 393224 | tf_op jit(solution)/shard_map/ppermute | solution.py:579
  27.9 14.5 %collective-permute-start.5 = (f32[256,128]{1,0:T(8,128)S(1)}, f32[256,128]{1,0:T(8,128)S(1)}, u32[]{:S(2)}, u32[]{:S(2)}) collective-permute-start(f32[256,128]{1,0:T(8,128)S(1)} %pad_maximum_fusion), channel_id=1, source_target_pairs={{1,0},{2,1},{3,2},{4,3},{5,4},{6,5},{7,6},{8,7},{9,8},{10,9},{11,1... | collective-permute-start | bytes 393224 | tf_op jit(solution)/shard_map/ppermute | solution.py:582
  42.4 0.1 stack.23
  42.5 0.0 collective-permute-done.near
  42.5 0.0 collective-permute-done.1.far
  42.5 5.6 %main.1 = (f32[10,4,32,128]{3,2,1,0:T(8,128)S(1)}, f32[4,4,32,128]{3,2,1,0:T(8,128)S(1)}, f32[2,3,128,128]{3,2,1,0:T(8,128)S(1)}, f32[36,32,128]{2,1,0:T(8,128)S(1)}) custom-call(f32[5]{0:T(128)S(1)} %convert_element_type.3.flags, bf16[2304,128]{1,0:T(8,128)(2,1)S(1)} %get-tuple-element.13.mine, bf16[2304,128]{1,0:T(8,128)(2,1)S(1)} %collective-permute-done.near, ...), custom_call_target="tpu_custom_call" | custom-call | flops 40000000 | bytes 4000000 | tf_op jit(solution)/shard_map/main/pallas_call | solution.py:529
  48.1 0.0 collective-permute-done.4.from_left
  48.1 0.0 collective-permute-done.5.from_right
  48.1 4.8 %finish.1 = (f32[4,128,128]{2,1,0:T(8,128)}, bf16[10,128,128]{2,1,0:T(8,128)(2,1)}, f32[128,128]{1,0:T(8,128)}) custom-call(f32[5]{0:T(128)S(1)} %convert_element_type.3.flags, f32[10,4,32,128]{3,2,1,0:T(8,128)S(1)} %get-tuple-element.15.two, f32[4,4,32,128]{3,2,1,0:T(8,128)S(1)} %get-tuple-element.16.ocean_two, ...), custom_call_target="tpu_custom_call" | custom-call | tf_op jit(solution)/shard_map/finish/pallas_call | solution.py:547
  (3 shorter events, 0.0 us)
Async XLA Ops:
  2.4 40.2 %collective-permute-start = (bf16[2304,128]{1,0:T(8,128)(2,1)S(1)}, bf16[2304,128]{1,0:T(8,128)(2,1)S(1)}, u32[]{:S(2)}, u32[]{:S(2)}) collective-permute-start(bf16[2304,128]{1,0:T(8,128)(2,1)S(1)} %get-tuple-element.13.mine), channel_id=1, source_target_pairs={{0,96},{96,0},{192,288},{288,192},{384,480},{480,384},{576,672},{6... | collective-permute-start | bytes 1769480 | tf_op jit(solution)/shard_map/ppermute | solution.py:592
  5.8 36.8 %collective-permute-start.1 = (bf16[2304,128]{1,0:T(8,128)(2,1)S(1)}, bf16[2304,128]{1,0:T(8,128)(2,1)S(1)}, u32[]{:S(2)}, u32[]{:S(2)}) collective-permute-start(bf16[2304,128]{1,0:T(8,128)(2,1)S(1)} %get-tuple-element.13.mine), channel_id=1, source_target_pairs={{96,192},{192,96},{288,384},{384,288},{480,576},{576,480},{97,193}... | collective-permute-start | bytes 1769480 | tf_op jit(solution)/shard_map/ppermute | solution.py:591
  10.6 10.2 %collective-permute-start.3 = (f32[128,128]{1,0:T(8,128)S(1)}, f32[128,128]{1,0:T(8,128)S(1)}, u32[]{:S(2)}, u32[]{:S(2)}) collective-permute-start(f32[128,128]{1,0:T(8,128)S(1)} %get-tuple-element.19), channel_id=1, source_target_pairs={{0,96},{96,0},{192,288},{288,192},{384,480},{480,384},{576,672},{6... | collective-permute-start | bytes 196616 | tf_op jit(solution)/shard_map/ppermute | solution.py:590
  12.5 13.5 %collective-permute-start.2 = (f32[128,128]{1,0:T(8,128)S(1)}, f32[128,128]{1,0:T(8,128)S(1)}, u32[]{:S(2)}, u32[]{:S(2)}) collective-permute-start(f32[128,128]{1,0:T(8,128)S(1)} %get-tuple-element.19), channel_id=1, source_target_pairs={{96,192},{192,96},{288,384},{384,288},{480,576},{576,480},{97,193}... | collective-permute-start | bytes 196616 | tf_op jit(solution)/shard_map/ppermute | solution.py:589
  26.0 22.1 %collective-permute-start.4 = (f32[256,128]{1,0:T(8,128)S(1)}, f32[256,128]{1,0:T(8,128)S(1)}, u32[]{:S(2)}, u32[]{:S(2)}) collective-permute-start(f32[256,128]{1,0:T(8,128)S(1)} %pad_maximum_fusion), channel_id=1, source_target_pairs={{0,1},{1,2},{2,3},{3,4},{4,5},{5,6},{6,7},{7,8},{8,9},{9,10},{10,1... | collective-permute-start | bytes 393224 | tf_op jit(solution)/shard_map/ppermute | solution.py:579
  27.9 20.2 %collective-permute-start.5 = (f32[256,128]{1,0:T(8,128)S(1)}, f32[256,128]{1,0:T(8,128)S(1)}, u32[]{:S(2)}, u32[]{:S(2)}) collective-permute-start(f32[256,128]{1,0:T(8,128)S(1)} %pad_maximum_fusion), channel_id=1, source_target_pairs={{1,0},{2,1},{3,2},{4,3},{5,4},{6,5},{7,6},{8,7},{9,8},{10,9},{11,1... | collective-permute-start | bytes 393224 | tf_op jit(solution)/shard_map/ppermute | solution.py:582
